TPU v7x, 256 devices: a whole 4x4x8 slice. The times are simulated.
256 devices in a mesh: pages: 64 (over x, z, core), query: 4 (over y).
Axes of the slice: x: 4, y: 4, z: 8, core: 2. Of those that a mesh axis runs over, the one named last changes fastest.
Arguments:
- queries: bfloat16 [64, 48, 32, 128], P('pages', 'query'), may hold values from -8 to 8
- pages: bfloat16 [1024, 1024, 128], P('pages', 'query'), may hold values from -8 to 8
- cand_owner: int32 [64, 24], P('pages'), may hold values from 0 to 63, all different within a row
- cand_slot: int32 [64, 24], P('pages'), may hold values from 0 to 15
Outputs:
- losses: float32 [64, 48], P('pages', 'query')
- query_grad: float32 [64, 48, 32, 128], P('pages', 'query')
- page_grad: float32 [1024, 1024, 128], P('pages', 'query')
Inputs may be any that keep to these rules, and one draw needn't show every extreme that they name: `cand_owner`: each row names 24 different owner indices, and every index is named by some row.
All inputs are finite; a program needn't handle non-finite values.
Results may differ from a plain program's by a relative error of at most 0.0024.
Values may be sent and summed in bfloat16 or wider, within the bound.
No kernel may reach another device: no remote copies, remote signals or barrier semaphores. Data moves between devices by JAX's collectives and lax.ppermute only.
A program may use at most 64 MiB of HBM per device.

v0:
```python
import jax
import jax.numpy as jnp
from jax import lax
from jax.sharding import PartitionSpec as P

SHARPNESS = 10.0
INV_TEMP = 20.0
LOSS_SCALE = 256.0
EPSILON = 1e-06


def from_everyone(value, axis):
    devices = lax.axis_size(axis)
    return lax.all_to_all(
        jnp.broadcast_to(value[None], (devices, *value.shape)), axis, 0, 0, tiled=True
    )


def joined_along(parts, dim):
    parts = jnp.moveaxis(parts, 0, dim)
    dims = parts.shape
    return parts.reshape(*dims[:dim], dims[dim] * dims[dim + 1], *dims[dim + 2 :])


def collect(value, axis, dim):
    parts = from_everyone(value, axis)
    return joined_along(parts, dim)


def over_copies(value, axis):
    return from_everyone(value, axis).sum(axis=0)


def normalize(embeddings):
    values = embeddings.astype(jnp.float32)
    inverse = lax.rsqrt(jnp.sum(values * values, axis=-1, keepdims=True) + EPSILON)
    return (values * inverse, inverse)


def unnormalize_grad(unit_vectors, inverse, gradient):
    return inverse * (
        gradient - unit_vectors * jnp.sum(unit_vectors * gradient, axis=-1, keepdims=True)
    )


def coefficients(totals, tokens):
    candidates = totals.shape[0]
    queries_here = totals.shape[1] // tokens
    shaped = totals.reshape(candidates, queries_here, tokens)
    per_token = jnp.log(shaped) / SHARPNESS
    logits = INV_TEMP * jnp.mean(per_token, axis=2)
    exponentials = jnp.exp(logits)
    denominator = jnp.sum(exponentials, axis=0)
    losses = jnp.log(denominator) - logits[0]
    positive = (jnp.arange(candidates) == 0).astype(jnp.float32)[:, None]
    probability = exponentials / denominator
    scaled = LOSS_SCALE * INV_TEMP / tokens * (probability - positive)
    weights = scaled[:, :, None] / shaped
    return (weights.reshape(candidates, queries_here * tokens), losses)


def local(queries, pages, cand_owner, cand_slot):
    queries_local = queries.shape[1]
    tokens = queries.shape[2]
    embed_width = queries.shape[3]
    owners_count = lax.axis_size("pages")
    q_unit, q_inv = normalize(queries[0])
    q_round = q_unit.astype(jnp.bfloat16).reshape(queries_local * tokens, embed_width)
    query_rows = collect(q_round, "query", 0)
    d_unit, d_inv = normalize(pages)
    d_round = d_unit.astype(jnp.bfloat16)
    owners = cand_owner[0]
    local_slots = cand_slot[0]
    owner_range = jnp.arange(owners_count, dtype=jnp.int32)
    wanted = jnp.sum(
        jnp.where(owners[None, :] == owner_range[:, None], local_slots[None, :], 0), axis=1
    )
    asked_slots = lax.all_to_all(wanted, "pages", split_axis=0, concat_axis=0, tiled=True)
    outgoing = jnp.take(d_round, asked_slots, axis=0)
    fetched = lax.all_to_all(outgoing, "pages", split_axis=0, concat_axis=0, tiled=True)
    chosen = jnp.take(fetched, owners, axis=0)

    def forward(unused, page_piece):
        scores = jnp.einsum("re,pe->rp", query_rows, page_piece, preferred_element_type=jnp.float32)
        return (unused, jnp.sum(jnp.exp(SHARPNESS * scores), axis=1))

    _, partial_value = lax.scan(forward, None, chosen)
    totals = over_copies(partial_value, "query")
    weights, losses_all = coefficients(totals, tokens)
    losses = lax.dynamic_slice_in_dim(
        losses_all, lax.axis_index("query") * queries_local, queries_local
    )

    def shares_of(page_piece, weight_row):
        scores = jnp.einsum("re,pe->rp", query_rows, page_piece, preferred_element_type=jnp.float32)
        return (weight_row[:, None] * jnp.exp(SHARPNESS * scores)).astype(jnp.bfloat16)

    start_rows = jnp.zeros((query_rows.shape[0], embed_width), jnp.float32)

    def page_side(unused, pair):
        page_piece, weight_row = pair
        shares = shares_of(page_piece, weight_row)
        return (
            unused,
            jnp.einsum("rp,re->pe", shares, query_rows, preferred_element_type=jnp.float32),
        )

    def query_side(grad_rows, pair):
        page_piece, weight_row = pair
        shares = shares_of(page_piece, weight_row)
        return (grad_rows + jnp.dot(shares, page_piece, preferred_element_type=jnp.float32), None)

    _, page_terms = lax.scan(page_side, None, (chosen, weights))
    grad_rows, _ = lax.scan(query_side, start_rows, (chosen, weights))
    candidates = owners.shape[0]
    selector = (owner_range[:, None] == owners[None, :]).astype(jnp.float32)
    returning = jnp.dot(
        selector, page_terms.reshape(candidates, -1), precision=lax.Precision.HIGHEST
    )
    returning = returning.reshape(owners_count, page_terms.shape[1], embed_width)
    returned = lax.all_to_all(returning, "pages", split_axis=0, concat_axis=0, tiled=True)
    own_grads = lax.psum_scatter(grad_rows, "query", scatter_dimension=0, tiled=True)
    query_grad = unnormalize_grad(
        q_unit, q_inv, own_grads.reshape(queries_local, tokens, embed_width)
    )
    page_range = jnp.arange(pages.shape[0], dtype=jnp.int32)
    picker = (page_range[:, None] == asked_slots[None, :]).astype(jnp.float32)
    summed = jnp.dot(picker, returned.reshape(owners_count, -1), precision=lax.Precision.HIGHEST)
    summed = summed.reshape(pages.shape[0], pages.shape[1], embed_width)
    page_grad = unnormalize_grad(d_unit, d_inv, summed)
    return (losses[None, :], query_grad[None], page_grad)


def solution(mesh):
    return jax.shard_map(
        local,
        mesh=mesh,
        in_specs=(
            P("pages", "query", None, None),
            P("pages", "query", None),
            P("pages", None),
            P("pages", None),
        ),
        out_specs=(P("pages", "query"), P("pages", "query", None, None), P("pages", "query", None)),
        check_vma=False,
    )
```

profile of v0, /device:TPU:1, one launch (start us, length us, event | category | flops | bytes accessed | tf_op | source)
XLA Modules:
  0.0 523.1 jit_solution(5002241479382218478)
XLA Ops:
  8.7 13.0 %all-to-all-start = ((s32[64,1,1]{2,1,0:T(1,128)}), s32[64,1,1]{2,1,0:T(1,128)S(1)}, u32[]{:S(2)}, u32[]{:S(2)}) async-start(s32[64,1,1]{2,1,0:T(1,128)} %copy.32), calls=%async_computation | async-start | bytes 65536 | tf_op jit(solution)/shard_map/all_to_all | solution.py:78
  23.7 2.9 fusion.41
  26.8 4.1 all-to-all-done
  32.2 3.1 gather_fusion
  35.3 4.6 broadcast_select_fusion
  39.9 6.5 %all-to-all-start.1 = ((bf16[64,256,128]{2,1,0:T(8,128)(2,1)}), bf16[64,256,128]{2,1,0:T(8,128)(2,1)}, u32[]{:S(2)}, u32[]{:S(2)}) async-start(bf16[64,256,128]{2,1,0:T(8,128)(2,1)} %broadcast_select_fusion), calls=%async_computation.1 | async-start | bytes 8388608 | tf_op jit(solution)/shard_map/all_to_all | solution.py:80
  46.8 95.5 %all-to-all-done.1 = bf16[64,256,128]{2,1,0:T(8,128)(2,1)} async-done(((bf16[64,256,128]{2,1,0:T(8,128)(2,1)}), bf16[64,256,128]{2,1,0:T(8,128)(2,1)}, u32[]{:S(2)}, u32[]{:S(2)}) %all-to-all-start.1) | async-done | bytes 4194336 | tf_op jit(solution)/shard_map/all_to_all | solution.py:80
  143.1 4.2 all-to-all-start.2
  147.3 3.0 gather_fusion.1
  151.7 3.2 all-to-all-done.2
  154.9 34.4 %while.31 = (s32[]{:T(128)}, f32[24,1536]{1,0:T(8,128)S(1)}, bf16[24,256,128]{2,1,0:T(8,128)(2,1)}, bf16[1536,128]{1,0:T(8,128)(2,1)S(1)}, s32[]{:T(128)}, /*index=5*/s32[]{:T(128)}) while((s32[]{:T(128)}, f32[24,1536]{1,0:T(8,128)S(1)}, bf16[24,256,128]{2,1,0:T(8,128)(2,1)}, bf16[1536,128]{1,0:T(8,128)(2,1)S(1)}, s32[]{:T(128)}, ...), condition=%wide.region_5.6_spmd, body=%wide.region_3.5_spmd.sunk | while | flops 101448192 | bytes 489557 | solution.py:87
  190.2 3.7 all-to-all-start.3
  193.9 8.4 %all-to-all-done.3 = f32[4,24,1536]{2,1,0:T(8,128)S(1)} async-done(((f32[4,24,1536]{2,1,0:T(8,128)}), f32[4,24,1536]{2,1,0:T(8,128)S(1)}, u32[]{:S(2)}, u32[]{:S(2)}) %all-to-all-start.3) | async-done | bytes 589856 | tf_op jit(solution)/shard_map/all_to_all | solution.py:14
  203.3 50.8 %while.32 = (s32[]{:T(128)}, f32[24,256,128]{2,1,0:T(8,128)}, f32[24,1536]{1,0:T(8,128)S(1)}, bf16[24,256,128]{2,1,0:T(8,128)(2,1)}, bf16[1536,128]{1,0:T(8,128)(2,1)S(1)}, /*index=5*/s32[]{:T(128)}) while((s32[]{:T(128)}, f32[24,256,128]{2,1,0:T(8,128)}, f32[24,1536]{1,0:T(8,128)S(1)}, bf16[24,256,128]{2,1,0:T(8,128)(2,1)}, ...), condition=%wide.region_14.15_spmd, body=%wide.region_13.14_spmd.sunk | while | flops 202506240 | bytes 1004625 | solution.py:113
  205.5 2.1 fusion.79
  207.6 2.1 fusion.79
  209.7 2.1 fusion.79
  211.8 2.1 fusion.79
  218.2 2.1 fusion.79
  222.4 2.1 fusion.79
  226.7 2.1 fusion.79
  235.1 2.1 fusion.79
  243.6 2.1 fusion.79
  247.8 2.1 fusion.79
  254.1 7.4 %fusion.36 = f32[64,256,128]{2,0,1:T(8,128)S(1)} fusion(s32[24]{0:T(128)S(1)} %bitcast.99, f32[3,8,256,128]{3,2,1,0:T(8,128)} %bitcast.95), kind=kOutput, calls=%fused_computation.41 | convolution fusion | flops 603981312 | bytes 11534432 | tf_op jit(solution)/shard_map/dot_general | solution.py:117
  261.6 8.1 %copy.36 = f32[64,256,128]{2,1,0:T(8,128)} copy(f32[64,256,128]{2,0,1:T(8,128)S(1)} %fusion.36) | data formatting | bytes 16777216 | tf_op jit(solution)/shard_map/dot_general | solution.py:117
  269.6 8.9 %all-to-all-start.4 = ((f32[64,256,128]{2,1,0:T(8,128)}), f32[64,256,128]{2,1,0:T(8,128)}, u32[]{:S(2)}, u32[]{:S(2)}) async-start(f32[64,256,128]{2,1,0:T(8,128)} %copy.36), calls=%async_computation.5 | async-start | bytes 16777216 | tf_op jit(solution)/shard_map/all_to_all | solution.py:121
  278.5 44.9 %while.33 = (s32[]{:T(128)}, f32[1536,128]{1,0:T(8,128)S(1)}, f32[24,1536]{1,0:T(8,128)S(1)}, bf16[24,256,128]{2,1,0:T(8,128)(2,1)}, bf16[1536,128]{1,0:T(8,128)(2,1)S(1)}, /*index=5*/s32[]{:T(128)}, s32[]{:T(128)}) while((s32[]{:T(128)}, f32[1536,128]{1,0:T(8,128)S(1)}, f32[24,1536]{1,0:T(8,128)S(1)}, ...), condition=%wide.region_10.11_spmd.clone, body=%wide.region_9.10_spmd.clone.sunk | while | flops 202899456 | bytes 2117218 | solution.py:114
  324.9 21.9 %reduce-scatter.2.cloned.1.call-done = f32[384,128]{1,0:T(8,128)} async-done(((f32[1536,128]{1,0:T(8,128)}), f32[384,128]{1,0:T(8,128)}) %reduce-scatter.2.cloned.1.call-update) | async-done | bytes 196624 | tf_op jit(solution)/shard_map/reduce_scatter | solution.py:122
  349.9 114.3 %all-to-all-done.4 = f32[64,256,128]{2,1,0:T(8,128)} async-done(((f32[64,256,128]{2,1,0:T(8,128)}), f32[64,256,128]{2,1,0:T(8,128)}, u32[]{:S(2)}, u32[]{:S(2)}) %all-to-all-start.4) | async-done | bytes 8388640 | tf_op jit(solution)/shard_map/all_to_all | solution.py:121
  464.2 10.6 %fusion.33 = f32[16,256,128]{2,0,1:T(8,128)S(1)} fusion(s32[64]{0:T(128)S(1)} %reduce.5, f32[8,8,256,128]{3,2,1,0:T(8,128)} %bitcast.26), kind=kOutput, calls=%fused_computation.36 | convolution fusion | flops 402654208 | bytes 10486016 | tf_op jit(solution)/shard_map/dot_general | solution.py:128
  474.8 39.4 %fusion.43 = f32[16,256,128]{2,0,1:T(8,128)S(1)} fusion(f32[16,256,128]{2,0,1:T(8,128)S(1)} %fusion.33, f32[16,256]{0,1:T(8,128)S(1)} %add_rsqrt_fusion, bf16[16,256,128]{2,1,0:T(8,128)(2,1)S(1)} %copy-done), kind=kOutput, calls=%fused_computation.50 | output fusion | flops 4198527 | bytes 5259264 | tf_op jit(solution)/shard_map/mul | solution.py:42
  (206 shorter events, 123.3 us)
Async XLA Ops:
  7.2 16.5 %copy-start = (bf16[16,256,128]{2,1,0:T(8,128)(2,1)S(1)}, bf16[16,256,128]{2,1,0:T(8,128)(2,1)}, u32[]{:S(2)}) copy-start(bf16[16,256,128]{2,1,0:T(8,128)(2,1)} %param.11) | copy-start | bytes 3145732
  8.7 22.2 %all-to-all-start = ((s32[64,1,1]{2,1,0:T(1,128)}), s32[64,1,1]{2,1,0:T(1,128)S(1)}, u32[]{:S(2)}, u32[]{:S(2)}) async-start(s32[64,1,1]{2,1,0:T(1,128)} %copy.32), calls=%async_computation | async-start | bytes 65536 | tf_op jit(solution)/shard_map/all_to_all | solution.py:78
  39.9 6.6 %copy-start.1 = (bf16[1,12,32,128]{3,2,1,0:T(8,128)(2,1)S(1)}, bf16[1,12,32,128]{3,2,1,0:T(8,128)(2,1)}, u32[]{:S(2)}) copy-start(bf16[1,12,32,128]{3,2,1,0:T(8,128)(2,1)} %param.10) | copy-start | bytes 294916
  39.9 6.8 %copy-start.3 = (s32[1,24]{1,0:T(1,128)S(1)}, s32[1,24]{1,0:T(1,128)}, u32[]{:S(2)}) copy-start(s32[1,24]{1,0:T(1,128)} %param.12) | copy-start | bytes 292
  39.9 102.4 %all-to-all-start.1 = ((bf16[64,256,128]{2,1,0:T(8,128)(2,1)}), bf16[64,256,128]{2,1,0:T(8,128)(2,1)}, u32[]{:S(2)}, u32[]{:S(2)}) async-start(bf16[64,256,128]{2,1,0:T(8,128)(2,1)} %broadcast_select_fusion), calls=%async_computation.1 | async-start | bytes 8388608 | tf_op jit(solution)/shard_map/all_to_all | solution.py:80
  143.1 11.8 %all-to-all-start.2 = ((bf16[4,384,128]{2,1,0:T(8,128)(2,1)}), bf16[4,384,128]{2,1,0:T(8,128)(2,1)S(1)}, u32[]{:S(2)}, u32[]{:S(2)}) async-start(bf16[4,384,128]{2,1,0:T(8,128)(2,1)} %broadcast_in_dim.87), calls=%async_computation.2 | async-start | bytes 786432 | tf_op jit(solution)/shard_map/all_to_all | solution.py:14
  190.2 12.0 %all-to-all-start.3 = ((f32[4,24,1536]{2,1,0:T(8,128)}), f32[4,24,1536]{2,1,0:T(8,128)S(1)}, u32[]{:S(2)}, u32[]{:S(2)}) async-start(f32[4,24,1536]{2,1,0:T(8,128)} %broadcast_in_dim.88), calls=%async_computation.3 | async-start | bytes 1179648 | tf_op jit(solution)/shard_map/all_to_all | solution.py:14
  269.6 194.6 %all-to-all-start.4 = ((f32[64,256,128]{2,1,0:T(8,128)}), f32[64,256,128]{2,1,0:T(8,128)}, u32[]{:S(2)}, u32[]{:S(2)}) async-start(f32[64,256,128]{2,1,0:T(8,128)} %copy.36), calls=%async_computation.5 | async-start | bytes 16777216 | tf_op jit(solution)/shard_map/all_to_all | solution.py:121
  278.5 68.4 %reduce-scatter.2.cloned.1.call-start = ((), (), s32[]{:S(2)}) async-start(), calls=%async_computation.6 | async-start | bytes 983040 | tf_op jit(solution)/shard_map/reduce_scatter | solution.py:122
  323.4 0.9 copy-start.2
Sparse Core Ops, SparseCore 0:
  324.4 22.3 reduce-scatter.1
where the time goes:
time: 527 us; the launch traced here: 523 us
  waiting for transfers between devices  247 us (47%)
  matrix products  141 us (27%)
  other arithmetic  55.9 us (11%)
  starting transfers between devices  36.2 us (7%)
  local copies, waits for them, and re-layouts  26.4 us (5%)
  between operations  14.3 us (3%)
    all_to_all x1, waiting for transfers between devices, local(): lax.all_to_all(returning, 'pages', split_axis=0, concat_axis=0, tiled=True)  114 us
    all_to_all x1, waiting for transfers between devices, local(): lax.all_to_all(outgoing, 'pages', split_axis=0, concat_axis=0, tiled=True)  95.5 us
    dot_general x24, matrix products, page_side(): jnp.einsum('rp,re->pe', shares, query_rows, preferred_element_type=jnp.fl...  50.1 us
    dot_general x24, matrix products, query_side(): jnp.dot(shares, page_piece, preferred_element_type=jnp.float32)  43.4 us
    mul x1, other arithmetic, unnormalize_grad(): unit_vectors * jnp.sum(unit_vectors * gradient, axis=-1, keepdims=True)  39.4 us
    dot_general x24, matrix products, forward(): jnp.einsum('re,pe->rp', query_rows, page_piece, preferred_element_type=jn...  29.5 us
    reduce_scatter x1, waiting for transfers between devices, local(): lax.psum_scatter(grad_rows, 'query', scatter_dimension=0, tiled=True)  21.9 us
    all_to_all x1, starting transfers between devices, local(): lax.all_to_all(wanted, 'pages', split_axis=0, concat_axis=0, tiled=True)  13 us
  transfers between devices with their start and end apart: 6, of which 6 were waited for; matrix products, arithmetic and copies ran while one was open for 11% of the time, Pallas kernels for 0%

commit v1 on v0

v1 whole, which is shorter than its diff:
```python
import functools
import math

import jax
import jax.numpy as jnp
from jax import lax
from jax.experimental import pallas as pl
from jax.experimental.pallas import tpu as pltpu
from jax.sharding import PartitionSpec as P

SHARPNESS = 10.0
INV_TEMP = 20.0
LOSS_SCALE = 256.0
EPSILON = 1e-06
EXP2_SCALE = SHARPNESS * math.log2(math.e)
PER_STEP = 4
GRAD_TYPE = jnp.bfloat16
OWN_TYPE = jnp.bfloat16


def exchange(value, axis):
    return lax.all_to_all(value, axis, split_axis=0, concat_axis=0, tiled=True)


def from_everyone(value, axis):
    devices = lax.axis_size(axis)
    return exchange(jnp.broadcast_to(value[None], (devices, *value.shape)), axis)


def normalize(embeddings):
    values = embeddings.astype(jnp.float32)
    inverse = lax.rsqrt(jnp.sum(values * values, axis=-1, keepdims=True) + EPSILON)
    return (values * inverse, inverse)


def unnormalize_grad(unit_vectors, inverse, gradient):
    return inverse * (
        gradient - unit_vectors * jnp.sum(unit_vectors * gradient, axis=-1, keepdims=True)
    )


def coefficients(totals, tokens):
    candidates = totals.shape[0]
    queries_here = totals.shape[1] // tokens
    shaped = totals.reshape(candidates, queries_here, tokens)
    per_token = jnp.log(shaped) / SHARPNESS
    logits = INV_TEMP * jnp.mean(per_token, axis=2)
    exponentials = jnp.exp(logits)
    denominator = jnp.sum(exponentials, axis=0)
    losses = jnp.log(denominator) - logits[0]
    positive = (jnp.arange(candidates) == 0).astype(jnp.float32)[:, None]
    probability = exponentials / denominator
    scaled = LOSS_SCALE * INV_TEMP / tokens * (probability - positive)
    weights = scaled[:, :, None] / shaped
    return (weights.reshape(candidates, queries_here * tokens), losses)


def patches_of(block, width):
    pieces = block.shape[1] // width
    return jnp.concatenate([block[:, j * width : (j + 1) * width] for j in range(pieces)], axis=0)


def row_chunk(rows):
    return 256 if rows % 256 == 0 else rows


def forward_kernel(width, q_ref, page_ref, totals_ref, unit_ref):
    per_step, pieces = page_ref.shape[0], page_ref.shape[1]
    patches = pieces * page_ref.shape[2] // width
    rows = q_ref.shape[0]
    chunk = row_chunk(rows)
    for c in range(per_step):
        unit, _ = normalize(patches_of(page_ref[c], width))
        unit_ref[c * patches : (c + 1) * patches, :] = unit.astype(jnp.bfloat16)
    for start in range(0, rows, chunk):
        block = q_ref[start : start + chunk, :]
        for c in range(per_step):
            scores = lax.dot_general(
                unit_ref[c * patches : (c + 1) * patches, :],
                block,
                (((1,), (1,)), ((), ())),
                preferred_element_type=jnp.float32,
            )
            sums = jnp.sum(jnp.exp2(scores * EXP2_SCALE), axis=0, keepdims=True)
            totals_ref[c, :, start : start + chunk] = sums


def backward_kernel(
    width, q_ref, page_ref, weight_ref, grad_ref, rows_ref, unit_ref, share_ref, back_ref
):
    per_step, pieces = page_ref.shape[0], page_ref.shape[1]
    patches = pieces * page_ref.shape[2] // width
    rows = q_ref.shape[0]
    chunk = row_chunk(rows)
    step = pl.program_id(0)
    for c in range(per_step):
        unit, _ = normalize(patches_of(page_ref[c], width))
        unit_ref[c * patches : (c + 1) * patches, :] = unit.astype(jnp.bfloat16)
    for start in range(0, rows, chunk):
        block = q_ref[start : start + chunk, :]
        for c in range(per_step):
            scores = lax.dot_general(
                unit_ref[c * patches : (c + 1) * patches, :],
                block,
                (((1,), (1,)), ((), ())),
                preferred_element_type=jnp.float32,
            )
            share = weight_ref[c, :, start : start + chunk] * jnp.exp2(scores * EXP2_SCALE)
            share_ref[c * patches : (c + 1) * patches, start : start + chunk] = share.astype(
                jnp.bfloat16
            )
    term = lax.dot_general(
        unit_ref[...], share_ref[...], (((0,), (0,)), ((), ())), preferred_element_type=jnp.float32
    )

    @pl.when(step == 0)
    def _():
        back_ref[...] = term

    @pl.when(step > 0)
    def _():
        back_ref[...] += term

    for c in range(per_step):
        gradient = jnp.dot(
            share_ref[c * patches : (c + 1) * patches, :],
            q_ref[...],
            preferred_element_type=jnp.float32,
        )
        unit, inverse = normalize(patches_of(page_ref[c], width))
        gradient = unnormalize_grad(unit, inverse, gradient).astype(grad_ref.dtype)
        for j in range(patches // pieces):
            grad_ref[c, :, j * width : (j + 1) * width] = gradient[j * pieces : (j + 1) * pieces, :]

    @pl.when(step == pl.num_programs(0) - 1)
    def _():
        rows_ref[...] = back_ref[...].T


def forward_totals(query_rows, chosen):
    rows, width = query_rows.shape
    candidates, pieces, wide = chosen.shape
    per_step = math.gcd(candidates, PER_STEP)
    patches = pieces * wide // width
    flops = 2 * candidates * patches * rows * width
    return pl.pallas_call(
        functools.partial(forward_kernel, width),
        grid=(candidates // per_step,),
        in_specs=[
            pl.BlockSpec((rows, width), lambda i: (0, 0)),
            pl.BlockSpec((per_step, pieces, wide), lambda i: (i, 0, 0)),
        ],
        out_specs=pl.BlockSpec((per_step, 1, rows), lambda i: (i, 0, 0)),
        out_shape=jax.ShapeDtypeStruct((candidates, 1, rows), jnp.float32),
        scratch_shapes=[pltpu.VMEM((per_step * patches, width), jnp.bfloat16)],
        cost_estimate=pl.CostEstimate(
            flops=flops,
            transcendentals=candidates * patches * rows,
            bytes_accessed=2 * candidates * patches * width,
        ),
        name="forward_totals",
    )(query_rows, chosen)


def backward_terms(query_rows, chosen, weights):
    rows, width = query_rows.shape
    candidates, pieces, wide = chosen.shape
    per_step = math.gcd(candidates, PER_STEP)
    patches = pieces * wide // width
    flops = 6 * candidates * patches * rows * width
    return pl.pallas_call(
        functools.partial(backward_kernel, width),
        grid=(candidates // per_step,),
        in_specs=[
            pl.BlockSpec((rows, width), lambda i: (0, 0)),
            pl.BlockSpec((per_step, pieces, wide), lambda i: (i, 0, 0)),
            pl.BlockSpec((per_step, 1, rows), lambda i: (i, 0, 0)),
        ],
        out_specs=[
            pl.BlockSpec((per_step, pieces, wide), lambda i: (i, 0, 0)),
            pl.BlockSpec((rows, width), lambda i: (0, 0)),
        ],
        out_shape=[
            jax.ShapeDtypeStruct(chosen.shape, GRAD_TYPE),
            jax.ShapeDtypeStruct((rows, width), jnp.float32),
        ],
        scratch_shapes=[
            pltpu.VMEM((per_step * patches, width), jnp.bfloat16),
            pltpu.VMEM((per_step * patches, rows), jnp.bfloat16),
            pltpu.VMEM((width, rows), jnp.float32),
        ],
        cost_estimate=pl.CostEstimate(
            flops=flops,
            transcendentals=candidates * patches * rows,
            bytes_accessed=4 * candidates * patches * width,
        ),
        name="backward_terms",
    )(query_rows, chosen, weights)


def local(queries, pages, cand_owner, cand_slot):
    queries_local, tokens, width = queries.shape[1:]
    local_pages, patches = pages.shape[:2]
    owners_count = lax.axis_size("pages")
    candidates = cand_owner.shape[1]
    rows_local = queries_local * tokens
    depth = patches // owners_count
    wide = depth * width
    pieces = pages.reshape(local_pages, depth, owners_count, width)
    spread = jnp.transpose(pieces, (2, 0, 1, 3)).reshape(owners_count, local_pages, wide)
    table = exchange(spread, "pages").reshape(owners_count * local_pages, wide)

    wanted = cand_owner[0] * local_pages + cand_slot[0]
    asked = from_everyone(wanted, "pages").reshape(owners_count * candidates)

    q_unit, q_inv = normalize(queries[0])
    q_round = q_unit.astype(jnp.bfloat16).reshape(rows_local, width)
    query_rows = from_everyone(q_round, "query").reshape(-1, width)

    page_range = jnp.arange(owners_count * local_pages, dtype=jnp.int32)
    picker = (asked[:, None] == page_range[None, :]).astype(jnp.bfloat16)
    served = jnp.dot(picker, table, preferred_element_type=jnp.float32).astype(jnp.bfloat16)
    fetched = exchange(served.reshape(owners_count, candidates, wide), "pages")
    chosen = jnp.transpose(fetched, (1, 0, 2))

    partial_totals = forward_totals(query_rows, chosen)
    totals = from_everyone(partial_totals.reshape(candidates, -1), "query").sum(axis=0)
    weights, losses_all = coefficients(totals, tokens)
    losses = lax.dynamic_slice_in_dim(
        losses_all, lax.axis_index("query") * queries_local, queries_local
    )

    page_terms, grad_rows = backward_terms(query_rows, chosen, weights[:, None, :])
    returned = exchange(jnp.transpose(page_terms, (1, 0, 2)), "pages")
    collector = (page_range[:, None] == asked[None, :]).astype(GRAD_TYPE)
    summed = jnp.dot(
        collector,
        returned.reshape(owners_count * candidates, wide),
        preferred_element_type=jnp.float32,
    )
    own = exchange(summed.astype(OWN_TYPE).reshape(owners_count, local_pages, wide), "pages")
    own = own.reshape(owners_count, local_pages, depth, width).astype(jnp.float32)
    page_grad = jnp.transpose(own, (1, 2, 0, 3)).reshape(pages.shape)

    own_grads = exchange(grad_rows.reshape(-1, rows_local, width), "query").sum(axis=0)
    query_grad = unnormalize_grad(
        q_unit, q_inv, own_grads.reshape(queries_local, tokens, width)
    )
    return (losses[None, :], query_grad[None], page_grad)


def solution(mesh):
    return jax.shard_map(
        local,
        mesh=mesh,
        in_specs=(
            P("pages", "query", None, None),
            P("pages", "query", None),
            P("pages", None),
            P("pages", None),
        ),
        out_specs=(P("pages", "query"), P("pages", "query", None, None), P("pages", "query", None)),
        check_vma=False,
    )
```

time: 527 us -> 268 us (0.51)
  matrix products: 141 us -> 5.77 us
  waiting for transfers between devices: 247 us -> 124 us
  other arithmetic: 55.9 us -> 3.98 us
  blocking collectives: 0 us -> 48.3 us
  Pallas kernels: 0 us -> 26.7 us
  between operations: 14.3 us -> 0.81 us
  local copies, waits for them, and re-layouts: 26.4 us -> 16.3 us
  starting transfers between devices: 36.2 us -> 41.9 us
    dot_general x74 -> x2, matrix products: 141 us -> 5.77 us  [the longest x1 3.01 us: local(): jnp.dot(picker, table, preferred_element_type=jnp.float32)]
    all_to_all x5 -> x7, waiting for transfers between devices: 226 us -> 124 us  [exchange(): return lax.all_to_all(value, axis, split_axis=0, concat_axis=0, tiled=True)]
    all_to_all x0 -> x1, blocking collectives: none -> 48.3 us  [exchange(): return lax.all_to_all(value, axis, split_axis=0, concat_axis=0, tiled=True)]
    mul x1 -> x0, other arithmetic: 39.4 us -> none  [unnormalize_grad(): unit_vectors * jnp.sum(unit_vectors * gradient, axis=-1, keepdims=True)]
    pallas_call x0 -> x2, Pallas kernels: none -> 26.7 us  [the longest x1 18.2 us: backward_terms(): pl.pallas_call(functools.partial(backward_kernel, width), grid=(candidate...]
    reduce_scatter x1 -> x0, waiting for transfers between devices: 21.9 us -> none  [local(): lax.psum_scatter(grad_rows, 'query', scatter_dimension=0, tiled=True)]
    dot_general x1 -> x0, local copies, waits for them, and re-layouts: 8.07 us -> none  [local(): jnp.dot(selector, page_terms.reshape(candidates, -1), precision=lax.Preci...]
    reshape x0 -> x4, local copies, waits for them, and re-layouts: none -> 6.47 us  [the longest x2 3.21 us: local(): page_grad = jnp.transpose(own, (1, 2, 0, 3)).reshape(pages.shape)]
  transfers between devices with their start and end apart: 6 -> 7, of which waited for: 6 -> 7; matrix products, arithmetic and copies ran while one was open for 11% -> 4% of each run, Pallas kernels for 0% -> 0%
where the time goes in v1:
time: 268 us; the launch traced here: 267 us
  waiting for transfers between devices  124 us (46%)
  blocking collectives  48.3 us (18%)
  starting transfers between devices  41.9 us (16%)
  Pallas kernels  26.7 us (10%)
  local copies, waits for them, and re-layouts  16.3 us (6%)
  matrix products  5.77 us (2%)
  other arithmetic  3.98 us (1%)
    all_to_all x7, waiting for transfers between devices, exchange(): return lax.all_to_all(value, axis, split_axis=0, concat_axis=0, tiled=True)  124 us
    all_to_all x1, blocking collectives, exchange(): return lax.all_to_all(value, axis, split_axis=0, concat_axis=0, tiled=True)  48.3 us
    all_to_all x7, starting transfers between devices, exchange(): return lax.all_to_all(value, axis, split_axis=0, concat_axis=0, tiled=True)  41.9 us
    pallas_call x1, Pallas kernels, backward_terms(): pl.pallas_call(functools.partial(backward_kernel, width), grid=(candidate...  18.2 us
    pallas_call x1, Pallas kernels, forward_totals(): pl.pallas_call(functools.partial(forward_kernel, width), grid=(candidates...  8.41 us
  transfers between devices with their start and end apart: 7, of which 7 were waited for; matrix products, arithmetic and copies ran while one was open for 4% of the time, Pallas kernels for 0%

profile of v1, /device:TPU:1, one launch (start us, length us, event | category | flops | bytes accessed | tf_op | source)
XLA Modules:
  0.0 267.3 jit_solution(6773710822999426609)
XLA Ops:
  1.9 13.0 %all-to-all-start.1 = ((s32[64,1,24]{2,1,0:T(1,128)}), s32[64,1,24]{2,1,0:T(1,128)S(1)}, u32[]{:S(2)}, u32[]{:S(2)}) async-start(s32[64,1,24]{2,1,0:T(1,128)} %broadcast_in_dim.11), calls=%async_computation.1 | async-start | bytes 65536 | tf_op jit(solution)/shard_map/all_to_all | solution.py:22
  14.9 2.0 copy.28
  17.0 1.2 reshape.156
  18.2 6.0 %all-to-all-done.1 = s32[64,1,24]{2,1,0:T(1,128)S(1)} async-done(((s32[64,1,24]{2,1,0:T(1,128)}), s32[64,1,24]{2,1,0:T(1,128)S(1)}, u32[]{:S(2)}, u32[]{:S(2)}) %all-to-all-start.1) | async-done | bytes 6176 | tf_op jit(solution)/shard_map/all_to_all | solution.py:22
  24.2 4.8 %all-to-all-start.2 = ((bf16[64,16,512]{2,1,0:T(8,128)(2,1)}), bf16[64,16,512]{2,1,0:T(8,128)(2,1)S(1)}, u32[]{:S(2)}, u32[]{:S(2)}) async-start(bf16[64,16,512]{2,1,0:T(8,128)(2,1)} %reshape.156), calls=%async_computation.2 | async-start | bytes 2097152 | tf_op jit(solution)/shard_map/all_to_all | solution.py:22
  29.4 0.7 reduce.6
  30.3 27.2 %all-to-all-done.2 = bf16[64,16,512]{2,1,0:T(8,128)(2,1)S(1)} async-done(((bf16[64,16,512]{2,1,0:T(8,128)(2,1)}), bf16[64,16,512]{2,1,0:T(8,128)(2,1)S(1)}, u32[]{:S(2)}, u32[]{:S(2)}) %all-to-all-start.2) | async-done | bytes 1048608 | tf_op jit(solution)/shard_map/all_to_all | solution.py:22
  57.5 3.0 %fusion.4 = bf16[1536,512]{1,0:T(8,128)(2,1)} fusion(bf16[1024,512]{1,0:T(8,128)(2,1)S(1)} %bitcast.45, s32[1536]{0:T(1024)S(1)} %eq.35), kind=kOutput, calls=%fused_computation.6 | convolution fusion | flops 1612972032 | bytes 2627584 | tf_op jit(solution)/shard_map/dot_general | solution.py:222
  60.5 6.4 %all-to-all-start.3 = ((bf16[64,24,512]{2,1,0:T(8,128)(2,1)}), bf16[64,24,512]{2,1,0:T(8,128)(2,1)S(1)}, u32[]{:S(2)}, u32[]{:S(2)}) async-start(bf16[64,24,512]{2,1,0:T(8,128)(2,1)} %bitcast.6), calls=%async_computation.3 | async-start | bytes 3145728 | tf_op jit(solution)/shard_map/all_to_all | solution.py:22
  67.3 39.4 %all-to-all-done.3 = bf16[64,24,512]{2,1,0:T(8,128)(2,1)S(1)} async-done(((bf16[64,24,512]{2,1,0:T(8,128)(2,1)}), bf16[64,24,512]{2,1,0:T(8,128)(2,1)S(1)}, u32[]{:S(2)}, u32[]{:S(2)}) %all-to-all-start.3) | async-done | bytes 1572896 | tf_op jit(solution)/shard_map/all_to_all | solution.py:22
  106.7 0.8 broadcast_in_dim.10
  107.5 4.2 %all-to-all-start = ((bf16[4,384,128]{2,1,0:T(8,128)(2,1)}), bf16[4,384,128]{2,1,0:T(8,128)(2,1)S(1)}, u32[]{:S(2)}, u32[]{:S(2)}) async-start(bf16[4,384,128]{2,1,0:T(8,128)(2,1)} %broadcast_in_dim.10), calls=%async_computation | async-start | bytes 786432 | tf_op jit(solution)/shard_map/all_to_all | solution.py:22
  111.6 1.6 copy.27
  113.3 6.2 %all-to-all-done = bf16[4,384,128]{2,1,0:T(8,128)(2,1)S(1)} async-done(((bf16[4,384,128]{2,1,0:T(8,128)(2,1)}), bf16[4,384,128]{2,1,0:T(8,128)(2,1)S(1)}, u32[]{:S(2)}, u32[]{:S(2)}) %all-to-all-start) | async-done | bytes 393248 | tf_op jit(solution)/shard_map/all_to_all | solution.py:22
  119.5 0.7 copy-done.1
  120.2 8.4 %forward_totals.1 = f32[24,1,1536]{2,1,0:T(1,128)} custom-call(bf16[1536,128]{1,0:T(8,128)(2,1)} %bitcast.47, bf16[24,64,512]{2,1,0:T(8,128)(2,1)} %bitcast.39), custom_call_target="tpu_custom_call" | custom-call | flops 2415919104 | bytes 1572864 | tf_op jit(solution)/shard_map/forward_totals/pallas_call | solution.py:146
  128.6 0.9 copy.29
  129.5 0.9 broadcast_in_dim.13
  130.4 3.7 %all-to-all-start.4 = ((f32[4,24,1536]{2,1,0:T(8,128)}), f32[4,24,1536]{2,1,0:T(8,128)S(1)}, u32[]{:S(2)}, u32[]{:S(2)}) async-start(f32[4,24,1536]{2,1,0:T(8,128)} %broadcast_in_dim.13), calls=%async_computation.4 | async-start | bytes 1179648 | tf_op jit(solution)/shard_map/all_to_all | solution.py:22
  134.1 8.5 %all-to-all-done.4 = f32[4,24,1536]{2,1,0:T(8,128)S(1)} async-done(((f32[4,24,1536]{2,1,0:T(8,128)}), f32[4,24,1536]{2,1,0:T(8,128)S(1)}, u32[]{:S(2)}, u32[]{:S(2)}) %all-to-all-start.4) | async-done | bytes 589856 | tf_op jit(solution)/shard_map/all_to_all | solution.py:22
  143.7 0.8 reshape_divide_fusion.weight_ref
  144.5 18.2 %backward_terms.1 = (bf16[24,64,512]{2,1,0:T(8,128)(2,1)}, f32[1536,128]{1,0:T(8,128)}) custom-call(bf16[1536,128]{1,0:T(8,128)(2,1)} %bitcast.48, bf16[24,64,512]{2,1,0:T(8,128)(2,1)} %bitcast.40, f32[24,1,1536]{2,1,0:T(1,128)} %reshape_divide_fusion.weight_ref), custom_call_target="tpu_custom_call" | custom-call | flops 7247757312 | bytes 3145728 | tf_op jit(solution)/shard_map/backward_terms/pallas_call | solution.py:171
  162.8 2.3 copy.21
  165.1 48.3 %all_to_all.41 = bf16[64,24,512]{2,1,0:T(8,128)(2,1)S(1)} all-to-all(bf16[64,24,512]{2,1,0:T(8,128)(2,1)S(1)} %copy.21), channel_id=1, replica_groups=mesh['pages'=64,'query'=4] {'pages'}, dimensions={0} | all-to-all | bytes 3145728 | tf_op jit(solution)/shard_map/all_to_all | solution.py:22
  213.4 3.5 %all-to-all-start.5 = ((f32[4,384,128]{2,1,0:T(8,128)}), f32[4,384,128]{2,1,0:T(8,128)S(1)}, u32[]{:S(2)}, u32[]{:S(2)}) async-start(f32[4,384,128]{2,1,0:T(8,128)} %bitcast.10), calls=%async_computation.5 | async-start | bytes 1572864 | tf_op jit(solution)/shard_map/all_to_all | solution.py:22
  216.9 2.8 %fusion.5 = bf16[1024,512]{1,0:T(8,128)(2,1)} fusion(bf16[1536,512]{1,0:T(8,128)(2,1)S(1)} %bitcast.41, s32[1536]{0:T(1024)S(1)} %eq.35), kind=kOutput, calls=%fused_computation.8 | convolution fusion | flops 1612709888 | bytes 2627584 | tf_op jit(solution)/shard_map/dot_general | solution.py:236
  219.7 9.5 %all-to-all-done.5 = f32[4,384,128]{2,1,0:T(8,128)S(1)} async-done(((f32[4,384,128]{2,1,0:T(8,128)}), f32[4,384,128]{2,1,0:T(8,128)S(1)}, u32[]{:S(2)}, u32[]{:S(2)}) %all-to-all-start.5) | async-done | bytes 786464 | tf_op jit(solution)/shard_map/all_to_all | solution.py:22
  229.2 6.4 %all-to-all-start.7 = ((bf16[64,16,512]{2,1,0:T(8,128)(2,1)}), bf16[64,16,512]{2,1,0:T(8,128)(2,1)S(1)}, u32[]{:S(2)}, u32[]{:S(2)}) async-start(bf16[64,16,512]{2,1,0:T(8,128)(2,1)} %bitcast.44), calls=%async_computation.7 | async-start | bytes 2097152 | tf_op jit(solution)/shard_map/all_to_all | solution.py:22
  236.5 0.8 subtract_multiply_fusion
  237.3 26.8 %all-to-all-done.7 = bf16[64,16,512]{2,1,0:T(8,128)(2,1)S(1)} async-done(((bf16[64,16,512]{2,1,0:T(8,128)(2,1)}), bf16[64,16,512]{2,1,0:T(8,128)(2,1)S(1)}, u32[]{:S(2)}, u32[]{:S(2)}) %all-to-all-start.7) | async-done | bytes 1048608 | tf_op jit(solution)/shard_map/all_to_all | solution.py:22
  264.1 0.7 reshape.170
  264.8 2.5 copy.22
  (24 shorter events, 4.2 us)
Async XLA Ops:
  1.9 22.2 %all-to-all-start.1 = ((s32[64,1,24]{2,1,0:T(1,128)}), s32[64,1,24]{2,1,0:T(1,128)S(1)}, u32[]{:S(2)}, u32[]{:S(2)}) async-start(s32[64,1,24]{2,1,0:T(1,128)} %broadcast_in_dim.11), calls=%async_computation.1 | async-start | bytes 65536 | tf_op jit(solution)/shard_map/all_to_all | solution.py:22
  24.2 33.3 %all-to-all-start.2 = ((bf16[64,16,512]{2,1,0:T(8,128)(2,1)}), bf16[64,16,512]{2,1,0:T(8,128)(2,1)S(1)}, u32[]{:S(2)}, u32[]{:S(2)}) async-start(bf16[64,16,512]{2,1,0:T(8,128)(2,1)} %reshape.156), calls=%async_computation.2 | async-start | bytes 2097152 | tf_op jit(solution)/shard_map/all_to_all | solution.py:22
  60.5 6.4 %copy-start = (bf16[1,12,32,128]{3,2,1,0:T(8,128)(2,1)S(1)}, bf16[1,12,32,128]{3,2,1,0:T(8,128)(2,1)}, u32[]{:S(2)}) copy-start(bf16[1,12,32,128]{3,2,1,0:T(8,128)(2,1)} %param.4) | copy-start | bytes 294916
  60.5 46.2 %all-to-all-start.3 = ((bf16[64,24,512]{2,1,0:T(8,128)(2,1)}), bf16[64,24,512]{2,1,0:T(8,128)(2,1)S(1)}, u32[]{:S(2)}, u32[]{:S(2)}) async-start(bf16[64,24,512]{2,1,0:T(8,128)(2,1)} %bitcast.6), calls=%async_computation.3 | async-start | bytes 3145728 | tf_op jit(solution)/shard_map/all_to_all | solution.py:22
  107.5 12.0 %all-to-all-start = ((bf16[4,384,128]{2,1,0:T(8,128)(2,1)}), bf16[4,384,128]{2,1,0:T(8,128)(2,1)S(1)}, u32[]{:S(2)}, u32[]{:S(2)}) async-start(bf16[4,384,128]{2,1,0:T(8,128)(2,1)} %broadcast_in_dim.10), calls=%async_computation | async-start | bytes 786432 | tf_op jit(solution)/shard_map/all_to_all | solution.py:22
  119.5 0.7 copy-start.1
  130.4 12.2 %all-to-all-start.4 = ((f32[4,24,1536]{2,1,0:T(8,128)}), f32[4,24,1536]{2,1,0:T(8,128)S(1)}, u32[]{:S(2)}, u32[]{:S(2)}) async-start(f32[4,24,1536]{2,1,0:T(8,128)} %broadcast_in_dim.13), calls=%async_computation.4 | async-start | bytes 1179648 | tf_op jit(solution)/shard_map/all_to_all | solution.py:22
  213.4 15.8 %all-to-all-start.5 = ((f32[4,384,128]{2,1,0:T(8,128)}), f32[4,384,128]{2,1,0:T(8,128)S(1)}, u32[]{:S(2)}, u32[]{:S(2)}) async-start(f32[4,384,128]{2,1,0:T(8,128)} %bitcast.10), calls=%async_computation.5 | async-start | bytes 1572864 | tf_op jit(solution)/shard_map/all_to_all | solution.py:22
  229.2 34.9 %all-to-all-start.7 = ((bf16[64,16,512]{2,1,0:T(8,128)(2,1)}), bf16[64,16,512]{2,1,0:T(8,128)(2,1)S(1)}, u32[]{:S(2)}, u32[]{:S(2)}) async-start(bf16[64,16,512]{2,1,0:T(8,128)(2,1)} %bitcast.44), calls=%async_computation.7 | async-start | bytes 2097152 | tf_op jit(solution)/shard_map/all_to_all | solution.py:22

commit v2 on v1

v2 whole, which is shorter than its diff:
```python
import functools
import math

import jax
import jax.numpy as jnp
from jax import lax
from jax.experimental import pallas as pl
from jax.experimental.pallas import tpu as pltpu
from jax.sharding import PartitionSpec as P

SHARPNESS = 10.0
INV_TEMP = 20.0
LOSS_SCALE = 256.0
EPSILON = 1e-06
EXP2_SCALE = SHARPNESS * math.log2(math.e)
PER_STEP = 4
GRAD_TYPE = jnp.bfloat16
OWN_TYPE = jnp.bfloat16


def exchange(value, axis):
    return lax.all_to_all(value, axis, split_axis=0, concat_axis=0, tiled=True)


def normalize(embeddings):
    values = embeddings.astype(jnp.float32)
    inverse = lax.rsqrt(jnp.sum(values * values, axis=-1, keepdims=True) + EPSILON)
    return (values * inverse, inverse)


def unnormalize_grad(unit_vectors, inverse, gradient):
    return inverse * (
        gradient - unit_vectors * jnp.sum(unit_vectors * gradient, axis=-1, keepdims=True)
    )


def coefficients(totals, tokens):
    candidates = totals.shape[0]
    queries_here = totals.shape[1] // tokens
    shaped = totals.reshape(candidates, queries_here, tokens)
    per_token = jnp.log(shaped) / SHARPNESS
    logits = INV_TEMP * jnp.mean(per_token, axis=2)
    exponentials = jnp.exp(logits)
    denominator = jnp.sum(exponentials, axis=0)
    losses = jnp.log(denominator) - logits[0]
    positive = (jnp.arange(candidates) == 0).astype(jnp.float32)[:, None]
    probability = exponentials / denominator
    scaled = LOSS_SCALE * INV_TEMP / tokens * (probability - positive)
    weights = scaled[:, :, None] / shaped
    return (weights.reshape(candidates, queries_here * tokens), losses)


def patches_of(block, width):
    pieces = block.shape[1] // width
    return jnp.concatenate([block[:, j * width : (j + 1) * width] for j in range(pieces)], axis=0)


def row_chunk(rows):
    return 256 if rows % 256 == 0 else rows


def units_of(page_ref, unit_ref, width):
    patches = page_ref.shape[1] * page_ref.shape[2] // width
    for c in range(page_ref.shape[0]):
        unit, _ = normalize(patches_of(page_ref[c], width))
        unit_ref[c * patches : (c + 1) * patches, :] = unit.astype(jnp.bfloat16)
    return patches


def exponentials_of(unit_block, row_block):
    scores = lax.dot_general(
        unit_block, row_block, (((1,), (1,)), ((), ())), preferred_element_type=jnp.float32
    )
    return jnp.exp2(scores * EXP2_SCALE)


def forward_kernel(width, q_ref, page_ref, totals_ref, unit_ref):
    per_step = page_ref.shape[0]
    patches = units_of(page_ref, unit_ref, width)
    rows = q_ref.shape[0]
    chunk = row_chunk(rows)
    first = pl.program_id(0) * per_step
    for start in range(0, rows, chunk):
        block = q_ref[start : start + chunk, :]
        for c in range(per_step):
            values = exponentials_of(unit_ref[c * patches : (c + 1) * patches, :], block)
            totals_ref[pl.ds(first + c, 1), start : start + chunk] = jnp.sum(
                values, axis=0, keepdims=True
            )


def fill_shares(q_ref, weight_ref, unit_ref, share_ref, per_step, patches):
    rows = q_ref.shape[0]
    chunk = row_chunk(rows)
    first = pl.program_id(0) * per_step
    for start in range(0, rows, chunk):
        block = q_ref[start : start + chunk, :]
        for c in range(per_step):
            values = exponentials_of(unit_ref[c * patches : (c + 1) * patches, :], block)
            weight = weight_ref[pl.ds(first + c, 1), start : start + chunk]
            share_ref[c * patches : (c + 1) * patches, start : start + chunk] = (
                weight * values
            ).astype(jnp.bfloat16)


def page_side_kernel(width, q_ref, page_ref, weight_ref, grad_ref, unit_ref, share_ref):
    per_step, pieces = page_ref.shape[0], page_ref.shape[1]
    patches = units_of(page_ref, unit_ref, width)
    fill_shares(q_ref, weight_ref, unit_ref, share_ref, per_step, patches)
    for c in range(per_step):
        gradient = jnp.dot(
            share_ref[c * patches : (c + 1) * patches, :],
            q_ref[...],
            preferred_element_type=jnp.float32,
        )
        unit, inverse = normalize(patches_of(page_ref[c], width))
        gradient = unnormalize_grad(unit, inverse, gradient).astype(grad_ref.dtype)
        for j in range(patches // pieces):
            grad_ref[c, :, j * width : (j + 1) * width] = gradient[j * pieces : (j + 1) * pieces, :]


def query_side_kernel(width, q_ref, page_ref, weight_ref, rows_ref, unit_ref, share_ref, back_ref):
    per_step = page_ref.shape[0]
    patches = units_of(page_ref, unit_ref, width)
    fill_shares(q_ref, weight_ref, unit_ref, share_ref, per_step, patches)
    step = pl.program_id(0)
    term = lax.dot_general(
        unit_ref[...], share_ref[...], (((0,), (0,)), ((), ())), preferred_element_type=jnp.float32
    )

    @pl.when(step == 0)
    def _():
        back_ref[...] = term

    @pl.when(step > 0)
    def _():
        back_ref[...] += term

    @pl.when(step == pl.num_programs(0) - 1)
    def _():
        rows_ref[...] = back_ref[...].T


def over_candidates(kernel, name, products, query_rows, chosen, weights, out_spec, out_shape, scratch):
    rows, width = query_rows.shape
    candidates, pieces, wide = chosen.shape
    per_step = math.gcd(candidates, PER_STEP)
    patches = pieces * wide // width
    table = pl.BlockSpec((candidates, rows), lambda i: (0, 0))
    return pl.pallas_call(
        functools.partial(kernel, width),
        grid=(candidates // per_step,),
        in_specs=[
            pl.BlockSpec((rows, width), lambda i: (0, 0)),
            pl.BlockSpec((per_step, pieces, wide), lambda i: (i, 0, 0)),
        ]
        + ([table] if weights else []),
        out_specs=out_spec or table,
        out_shape=out_shape,
        scratch_shapes=[pltpu.VMEM((per_step * patches, width), jnp.bfloat16)] + scratch,
        cost_estimate=pl.CostEstimate(
            flops=2 * products * candidates * patches * rows * width,
            transcendentals=candidates * patches * rows,
            bytes_accessed=4 * candidates * patches * width,
        ),
        name=name,
    )(query_rows, chosen, *weights)


def forward_totals(query_rows, chosen):
    shape = jax.ShapeDtypeStruct((chosen.shape[0], query_rows.shape[0]), jnp.float32)
    return over_candidates(
        forward_kernel, "forward_totals", 1, query_rows, chosen, [], None, shape, []
    )


def share_scratch(query_rows, chosen):
    per_step = math.gcd(chosen.shape[0], PER_STEP)
    patches = chosen.shape[1] * chosen.shape[2] // query_rows.shape[1]
    return pltpu.VMEM((per_step * patches, query_rows.shape[0]), jnp.bfloat16)


def page_side(query_rows, chosen, weights):
    per_step = math.gcd(chosen.shape[0], PER_STEP)
    return over_candidates(
        page_side_kernel,
        "page_side",
        2,
        query_rows,
        chosen,
        [weights],
        pl.BlockSpec((per_step, *chosen.shape[1:]), lambda i: (i, 0, 0)),
        jax.ShapeDtypeStruct(chosen.shape, GRAD_TYPE),
        [share_scratch(query_rows, chosen)],
    )


def query_side(query_rows, chosen, weights):
    return over_candidates(
        query_side_kernel,
        "query_side",
        2,
        query_rows,
        chosen,
        [weights],
        pl.BlockSpec(query_rows.shape, lambda i: (0, 0)),
        jax.ShapeDtypeStruct(query_rows.shape, jnp.float32),
        [
            share_scratch(query_rows, chosen),
            pltpu.VMEM((query_rows.shape[1], query_rows.shape[0]), jnp.float32),
        ],
    )


def from_ahead(value, axis, shift):
    devices = lax.axis_size(axis)
    pairs = [((i + shift) % devices, i) for i in range(devices)]
    return lax.ppermute(value, axis, pairs)


def gathered(value, axis):
    devices = lax.axis_size(axis)
    me = lax.axis_index(axis)
    parts, stride = value[None], 1
    for factor in factors(devices):
        place = (me // stride) % factor
        received = [parts]
        for shift in range(1, factor):
            pairs = []
            for i in range(devices):
                ahead = (i // stride + shift) % factor
                pairs.append((i + (ahead - (i // stride) % factor) * stride, i))
            received.append(lax.ppermute(parts, axis, pairs))
        ahead_first = jnp.stack(received)
        ordered = jnp.roll(ahead_first, place, axis=0) if factor > 1 else ahead_first
        parts = ordered.reshape(-1, *value.shape)
        stride *= factor
    return parts


def factors(devices):
    return [f for f in (2, devices // 8, 4) if f > 1] if devices >= 16 else [devices]


def local(queries, pages, cand_owner, cand_slot):
    queries_local, tokens, width = queries.shape[1:]
    local_pages, patches = pages.shape[:2]
    owners_count = lax.axis_size("pages")
    group = lax.axis_size("query")
    candidates = cand_owner.shape[1]
    rows_local = queries_local * tokens
    depth = patches // owners_count
    wide = depth * width
    pieces = pages.reshape(local_pages, depth, owners_count, width)
    spread = jnp.transpose(pieces, (2, 0, 1, 3)).reshape(owners_count, local_pages, wide)
    table = exchange(spread, "pages").reshape(owners_count * local_pages, wide)

    wanted = cand_owner[0] * local_pages + cand_slot[0]
    asked = gathered(wanted, "pages").reshape(owners_count * candidates)

    q_unit, q_inv = normalize(queries[0])
    q_round = q_unit.astype(jnp.bfloat16).reshape(rows_local, width)
    query_rows = jnp.concatenate(
        [q_round] + [from_ahead(q_round, "query", k) for k in range(1, group)], axis=0
    )

    page_range = jnp.arange(owners_count * local_pages, dtype=jnp.int32)
    picker = (asked[:, None] == page_range[None, :]).astype(jnp.bfloat16)
    served = jnp.dot(picker, table, preferred_element_type=jnp.float32).astype(jnp.bfloat16)
    fetched = exchange(served.reshape(owners_count, candidates, wide), "pages")
    chosen = jnp.transpose(fetched, (1, 0, 2))

    partial_totals = forward_totals(query_rows, chosen)
    totals = partial_totals
    for k in range(1, group):
        theirs = from_ahead(partial_totals, "query", k)
        totals = totals + jnp.roll(theirs, k * rows_local, axis=1)
    weights, losses_all = coefficients(totals, tokens)
    losses = losses_all[:queries_local]

    page_terms = page_side(query_rows, chosen, weights)
    returned = exchange(jnp.transpose(page_terms, (1, 0, 2)), "pages")
    collector = (page_range[:, None] == asked[None, :]).astype(GRAD_TYPE)
    summed = jnp.dot(
        collector,
        returned.reshape(owners_count * candidates, wide),
        preferred_element_type=jnp.float32,
    )
    own = exchange(summed.astype(OWN_TYPE).reshape(owners_count, local_pages, wide), "pages")
    own = own.reshape(owners_count, local_pages, depth, width).astype(jnp.float32)
    page_grad = jnp.transpose(own, (1, 2, 0, 3)).reshape(pages.shape)

    grad_rows = query_side(query_rows, chosen, weights).reshape(group, rows_local, width)
    own_grads = grad_rows[0]
    for k in range(1, group):
        own_grads = own_grads + from_ahead(grad_rows[k], "query", group - k)
    query_grad = unnormalize_grad(
        q_unit, q_inv, own_grads.reshape(queries_local, tokens, width)
    )
    return (losses[None, :], query_grad[None], page_grad)


def solution(mesh):
    return jax.shard_map(
        local,
        mesh=mesh,
        in_specs=(
            P("pages", "query", None, None),
            P("pages", "query", None),
            P("pages", None),
            P("pages", None),
        ),
        out_specs=(P("pages", "query"), P("pages", "query", None, None), P("pages", "query", None)),
        check_vma=False,
    )
```

time: 268 us -> 237 us (0.88)
  waiting for transfers between devices: 124 us -> 69.2 us
  starting transfers between devices: 41.9 us -> 60.8 us
  Pallas kernels: 26.7 us -> 35.9 us
  local copies, waits for them, and re-layouts: 16.3 us -> 13.1 us
    all_to_all x7 -> x3, waiting for transfers between devices: 124 us -> 30.1 us  [exchange(): return lax.all_to_all(value, axis, split_axis=0, concat_axis=0, tiled=True)]
    ppermute x0 -> x20, waiting for transfers between devices: none -> 39.1 us  [the longest x9 21.1 us: from_ahead(): return lax.ppermute(value, axis, pairs)]
    ppermute x0 -> x20, starting transfers between devices: none -> 30.4 us  [the longest x11 18.1 us: gathered(): received.append(lax.ppermute(parts, axis, pairs))]
    all_to_all x7 -> x3, starting transfers between devices: 41.9 us -> 30.4 us  [exchange(): return lax.all_to_all(value, axis, split_axis=0, concat_axis=0, tiled=True)]
    pallas_call x2 -> x3, Pallas kernels: 26.7 us -> 35.9 us  [over_candidates(): pl.pallas_call(functools.partial(kernel, width), grid=(candidates // per_...]
  transfers between devices with their start and end apart: 7 -> 23, of which waited for: 7 -> 14; matrix products, arithmetic and copies ran while one was open for 4% -> 2% of each run, Pallas kernels for 0% -> 6%
where the time goes in v2:
time: 237 us
  waiting for transfers between devices  69.2 us (29%)
  starting transfers between devices  60.8 us (26%)
  blocking collectives  46 us (19%)
  Pallas kernels  35.9 us (15%)
  local copies, waits for them, and re-layouts  13.1 us (6%)
  matrix products  5.8 us (2%)
  other arithmetic  5.07 us (2%)
    all_to_all x1, blocking collectives, exchange(): return lax.all_to_all(value, axis, split_axis=0, concat_axis=0, tiled=True)  46 us
    pallas_call x3, Pallas kernels, over_candidates(): pl.pallas_call(functools.partial(kernel, width), grid=(candidates // per_...  35.9 us
    all_to_all x3, starting transfers between devices, exchange(): return lax.all_to_all(value, axis, split_axis=0, concat_axis=0, tiled=True)  30.4 us
    all_to_all x3, waiting for transfers between devices, exchange(): return lax.all_to_all(value, axis, split_axis=0, concat_axis=0, tiled=True)  30.1 us
    ppermute x9, waiting for transfers between devices, from_ahead(): return lax.ppermute(value, axis, pairs)  21.1 us
    ppermute x11, starting transfers between devices, gathered(): received.append(lax.ppermute(parts, axis, pairs))  18.1 us
    ppermute x11, waiting for transfers between devices, gathered(): received.append(lax.ppermute(parts, axis, pairs))  18 us
    ppermute x9, starting transfers between devices, from_ahead(): return lax.ppermute(value, axis, pairs)  12.3 us
  transfers between devices with their start and end apart: 23, of which 14 were waited for; matrix products, arithmetic and copies ran while one was open for 2% of the time, Pallas kernels for 6%

profile of v2, /device:TPU:1, one launch (start us, length us, event | category | flops | bytes accessed | tf_op | source)
XLA Modules:
  0.0 236.8 jit_solution(2041476502432158221)
XLA Ops:
  0.6 2.0 copy.19
  3.9 13.1 %all-to-all-start = ((bf16[64,16,512]{2,1,0:T(8,128)(2,1)}), bf16[64,16,512]{2,1,0:T(8,128)(2,1)S(1)}, u32[]{:S(2)}, u32[]{:S(2)}) async-start(bf16[64,16,512]{2,1,0:T(8,128)(2,1)} %reshape.147), calls=%async_computation | async-start | bytes 2097152 | tf_op jit(solution)/shard_map/all_to_all | solution.py:22
  18.4 2.6 %collective-permute-start.4 = (s32[2,24]{1,0:T(2,128)S(1)}, s32[2,24]{1,0:T(2,128)S(1)}, u32[]{:S(2)}, u32[]{:S(2)}) collective-permute-start(s32[2,24]{1,0:T(2,128)S(1)} %bitcast.85), channel_id=1, source_target_pairs={{8,0},{12,4},{16,8},{20,12},{24,16},{28,20},{32,24},{36,28},{40,32... | collective-permute-start | bytes 584 | tf_op jit(solution)/shard_map/ppermute | solution.py:233
  21.0 2.1 collective-permute-start.5
  24.3 3.3 %collective-permute-start.7 = (s32[2,24]{1,0:T(2,128)S(1)}, s32[2,24]{1,0:T(2,128)S(1)}, u32[]{:S(2)}, u32[]{:S(2)}) collective-permute-start(s32[2,24]{1,0:T(2,128)S(1)} %bitcast.88), channel_id=1, source_target_pairs={{32,0},{36,4},{40,8},{44,12},{48,16},{52,20},{56,24},{60,28},{0,32... | collective-permute-start | bytes 584 | tf_op jit(solution)/shard_map/ppermute | solution.py:233
  27.6 13.5 %collective-permute-done.4 = s32[2,24]{1,0:T(2,128)S(1)} collective-permute-done((s32[2,24]{1,0:T(2,128)S(1)}, s32[2,24]{1,0:T(2,128)S(1)}, u32[]{:S(2)}, u32[]{:S(2)}) %collective-permute-start.4) | collective-permute-done | bytes 224 | tf_op jit(solution)/shard_map/ppermute | solution.py:233
  41.1 4.7 %collective-permute-start.10 = (s32[2,24]{1,0:T(2,128)S(1)}, s32[2,24]{1,0:T(2,128)S(1)}, u32[]{:S(2)}, u32[]{:S(2)}) collective-permute-start(s32[2,24]{1,0:T(2,128)S(1)} %bitcast.92), channel_id=1, source_target_pairs={{56,0},{60,4},{0,8},{4,12},{8,16},{12,20},{16,24},{20,28},{24,32},... | collective-permute-start | bytes 584 | tf_op jit(solution)/shard_map/ppermute | solution.py:233
  46.6 2.7 %collective-permute-start.11 = (s32[16,24]{1,0:T(8,128)S(1)}, s32[16,24]{1,0:T(8,128)S(1)}, u32[]{:S(2)}, u32[]{:S(2)}) collective-permute-start(s32[16,24]{1,0:T(8,128)S(1)} %bitcast.80), channel_id=1, source_target_pairs={{64,0},{68,4},{72,8},{76,12},{80,16},{84,20},{88,24},{92,28},{96,3... | collective-permute-start | bytes 4616 | tf_op jit(solution)/shard_map/ppermute | solution.py:233
  50.3 3.0 %collective-permute-done.12 = s32[16,24]{1,0:T(8,128)S(1)} collective-permute-done((s32[16,24]{1,0:T(8,128)S(1)}, s32[16,24]{1,0:T(8,128)S(1)}, u32[]{:S(2)}, u32[]{:S(2)}) %collective-permute-start.12) | collective-permute-done | bytes 1568 | tf_op jit(solution)/shard_map/ppermute | solution.py:233
  53.5 3.0 %fusion.4 = bf16[1536,512]{1,0:T(8,128)(2,1)} fusion(bf16[1024,512]{1,0:T(8,128)(2,1)S(1)} %bitcast.78, s32[1536]{0:T(1024)S(1)} %eq.46), kind=kOutput, calls=%fused_computation.6 | convolution fusion | flops 1612972032 | bytes 2627584 | tf_op jit(solution)/shard_map/dot_general | solution.py:269
  56.5 11.2 %all-to-all-start.1 = ((bf16[64,24,512]{2,1,0:T(8,128)(2,1)}), bf16[64,24,512]{2,1,0:T(8,128)(2,1)S(1)}, u32[]{:S(2)}, u32[]{:S(2)}) async-start(bf16[64,24,512]{2,1,0:T(8,128)(2,1)} %bitcast.20), calls=%async_computation.1 | async-start | bytes 3145728 | tf_op jit(solution)/shard_map/all_to_all | solution.py:22
  68.0 1.4 collective-permute-start.2
  69.4 2.6 %collective-permute-start.1 = (bf16[384,128]{1,0:T(8,128)(2,1)S(1)}, bf16[384,128]{1,0:T(8,128)(2,1)S(1)}, u32[]{:S(2)}, u32[]{:S(2)}) collective-permute-start(bf16[384,128]{1,0:T(8,128)(2,1)S(1)} %fusion.8), channel_id=1, source_target_pairs={{2,0},{3,1},{0,2},{1,3},{6,4},{7,5},{4,6},{5,7},{10,8},{11,9},{8,1... | collective-permute-start | bytes 294920 | tf_op jit(solution)/shard_map/ppermute | solution.py:218
  73.4 3.2 %collective-permute-done.1 = bf16[384,128]{1,0:T(8,128)(2,1)S(1)} collective-permute-done((bf16[384,128]{1,0:T(8,128)(2,1)S(1)}, bf16[384,128]{1,0:T(8,128)(2,1)S(1)}, u32[]{:S(2)}, u32[]{:S(2)}) %collective-permute-start.1) | collective-permute-done | bytes 98336 | tf_op jit(solution)/shard_map/ppermute | solution.py:218
  77.4 30.1 %all-to-all-done.1 = bf16[64,24,512]{2,1,0:T(8,128)(2,1)S(1)} async-done(((bf16[64,24,512]{2,1,0:T(8,128)(2,1)}), bf16[64,24,512]{2,1,0:T(8,128)(2,1)S(1)}, u32[]{:S(2)}, u32[]{:S(2)}) %all-to-all-start.1) | async-done | bytes 1572896 | tf_op jit(solution)/shard_map/all_to_all | solution.py:22
  107.4 1.6 copy.18
  109.1 8.5 %forward_totals.1 = f32[24,1536]{1,0:T(8,128)} custom-call(bf16[1536,128]{1,0:T(8,128)(2,1)} %pad_maximum_fusion.q_ref, bf16[24,64,512]{2,1,0:T(8,128)(2,1)} %bitcast.72), custom_call_target="tpu_custom_call" | custom-call | flops 2415919104 | bytes 3145728 | tf_op jit(solution)/shard_map/forward_totals/pallas_call | solution.py:150
  118.9 1.4 collective-permute-start.14
  120.3 1.6 collective-permute-start.15
  122.0 2.5 %collective-permute-done.16 = f32[24,1536]{1,0:T(8,128)S(1)} collective-permute-done((f32[24,1536]{1,0:T(8,128)}, f32[24,1536]{1,0:T(8,128)S(1)}, u32[]{:S(2)}, u32[]{:S(2)}) %collective-permute-start.16) | collective-permute-done | bytes 147488 | tf_op jit(solution)/shard_map/ppermute | solution.py:218
  124.5 4.2 %collective-permute-done.15 = f32[24,1536]{1,0:T(8,128)S(1)} collective-permute-done((f32[24,1536]{1,0:T(8,128)}, f32[24,1536]{1,0:T(8,128)S(1)}, u32[]{:S(2)}, u32[]{:S(2)}) %collective-permute-start.15) | collective-permute-done | bytes 147488 | tf_op jit(solution)/shard_map/ppermute | solution.py:218
  131.4 14.0 %page_side.1 = bf16[24,64,512]{2,1,0:T(8,128)(2,1)} custom-call(bf16[1536,128]{1,0:T(8,128)(2,1)} %pad_maximum_fusion.q_ref, bf16[24,64,512]{2,1,0:T(8,128)(2,1)} %bitcast.73, f32[24,1536]{1,0:T(8,128)} %div.62.weight_ref), custom_call_target="tpu_custom_call" | custom-call | flops 4831838208 | bytes 3145728 | tf_op jit(solution)/shard_map/page_side/pallas_call | solution.py:150
  145.4 2.3 copy.14
  147.7 46.0 %all_to_all.20 = bf16[64,24,512]{2,1,0:T(8,128)(2,1)S(1)} all-to-all(bf16[64,24,512]{2,1,0:T(8,128)(2,1)S(1)} %copy.14), channel_id=1, replica_groups=mesh['pages'=64,'query'=4] {'pages'}, dimensions={0} | all-to-all | bytes 3145728 | tf_op jit(solution)/shard_map/all_to_all | solution.py:22
  193.7 2.8 %fusion.5 = bf16[1024,512]{1,0:T(8,128)(2,1)} fusion(bf16[1536,512]{1,0:T(8,128)(2,1)S(1)} %bitcast.75, s32[1536]{0:T(1024)S(1)} %eq.46), kind=kOutput, calls=%fused_computation.8 | convolution fusion | flops 1612709888 | bytes 2627584 | tf_op jit(solution)/shard_map/dot_general | solution.py:284
  196.5 6.1 %all-to-all-start.3 = ((bf16[64,16,512]{2,1,0:T(8,128)(2,1)}), bf16[64,16,512]{2,1,0:T(8,128)(2,1)S(1)}, u32[]{:S(2)}, u32[]{:S(2)}) async-start(bf16[64,16,512]{2,1,0:T(8,128)(2,1)} %bitcast.27), calls=%async_computation.3 | async-start | bytes 2097152 | tf_op jit(solution)/shard_map/all_to_all | solution.py:22
  202.6 13.4 %query_side.1 = f32[1536,128]{1,0:T(8,128)} custom-call(bf16[1536,128]{1,0:T(8,128)(2,1)} %pad_maximum_fusion.q_ref, bf16[24,64,512]{2,1,0:T(8,128)(2,1)} %bitcast.74, f32[24,1536]{1,0:T(8,128)} %div.62.weight_ref), custom_call_target="tpu_custom_call" | custom-call | flops 4831838208 | bytes 3145728 | tf_op jit(solution)/shard_map/query_side/pallas_call | solution.py:150
  217.1 1.8 collective-permute-start.19
  220.5 2.7 %collective-permute-done.19 = f32[384,128]{1,0:T(8,128)S(1)} collective-permute-done((f32[384,128]{1,0:T(8,128)S(1)}, f32[384,128]{1,0:T(8,128)S(1)}, u32[]{:S(2)}, u32[]{:S(2)}) %collective-permute-start.19) | collective-permute-done | bytes 196640 | tf_op jit(solution)/shard_map/ppermute | solution.py:218
  223.2 3.0 %collective-permute-done.18 = f32[384,128]{1,0:T(8,128)S(1)} collective-permute-done((f32[384,128]{1,0:T(8,128)S(1)}, f32[384,128]{1,0:T(8,128)S(1)}, u32[]{:S(2)}, u32[]{:S(2)}) %collective-permute-start.18) | collective-permute-done | bytes 196640 | tf_op jit(solution)/shard_map/ppermute | solution.py:218
  226.2 5.3 %collective-permute-done.17 = f32[384,128]{1,0:T(8,128)S(1)} collective-permute-done((f32[384,128]{1,0:T(8,128)S(1)}, f32[384,128]{1,0:T(8,128)S(1)}, u32[]{:S(2)}, u32[]{:S(2)}) %collective-permute-start.17) | collective-permute-done | bytes 196640 | tf_op jit(solution)/shard_map/ppermute | solution.py:218
  234.2 2.5 %copy.15 = f32[64,16,4,128]{3,0,2,1:T(8,128)} copy(f32[64,16,4,128]{3,2,1,0:T(4,128)S(1)} %reshape.160) | data formatting | bytes 4194304 | tf_op jit(solution)/shard_map/reshape | solution.py:291
  (86 shorter events, 17.8 us)
Async XLA Ops:
  3.9 13.1 %copy-start.1 = (s32[1,24]{1,0:T(1,128)S(1)}, s32[1,24]{1,0:T(1,128)}, u32[]{:S(2)}) copy-start(s32[1,24]{1,0:T(1,128)} %param.7) | copy-start | bytes 292
  3.9 13.1 %copy-start.2 = (s32[1,24]{1,0:T(1,128)S(1)}, s32[1,24]{1,0:T(1,128)}, u32[]{:S(2)}) copy-start(s32[1,24]{1,0:T(1,128)} %param.6) | copy-start | bytes 292
  3.9 49.6 %all-to-all-start = ((bf16[64,16,512]{2,1,0:T(8,128)(2,1)}), bf16[64,16,512]{2,1,0:T(8,128)(2,1)S(1)}, u32[]{:S(2)}, u32[]{:S(2)}) async-start(bf16[64,16,512]{2,1,0:T(8,128)(2,1)} %reshape.147), calls=%async_computation | async-start | bytes 2097152 | tf_op jit(solution)/shard_map/all_to_all | solution.py:22
  17.0 1.4 collective-permute-start.3
  18.4 22.6 %collective-permute-start.4 = (s32[2,24]{1,0:T(2,128)S(1)}, s32[2,24]{1,0:T(2,128)S(1)}, u32[]{:S(2)}, u32[]{:S(2)}) collective-permute-start(s32[2,24]{1,0:T(2,128)S(1)} %bitcast.85), channel_id=1, source_target_pairs={{8,0},{12,4},{16,8},{20,12},{24,16},{28,20},{32,24},{36,28},{40,32... | collective-permute-start | bytes 584 | tf_op jit(solution)/shard_map/ppermute | solution.py:233
  21.0 20.1 %collective-permute-start.5 = (s32[2,24]{1,0:T(2,128)S(1)}, s32[2,24]{1,0:T(2,128)S(1)}, u32[]{:S(2)}, u32[]{:S(2)}) collective-permute-start(s32[2,24]{1,0:T(2,128)S(1)} %bitcast.86), channel_id=1, source_target_pairs={{16,0},{20,4},{24,8},{28,12},{32,16},{36,20},{40,24},{44,28},{48,3... | collective-permute-start | bytes 584 | tf_op jit(solution)/shard_map/ppermute | solution.py:233
  23.1 22.7 %collective-permute-start.6 = (s32[2,24]{1,0:T(2,128)S(1)}, s32[2,24]{1,0:T(2,128)S(1)}, u32[]{:S(2)}, u32[]{:S(2)}) collective-permute-start(s32[2,24]{1,0:T(2,128)S(1)} %bitcast.87), channel_id=1, source_target_pairs={{24,0},{28,4},{32,8},{36,12},{40,16},{44,20},{48,24},{52,28},{56,3... | collective-permute-start | bytes 584 | tf_op jit(solution)/shard_map/ppermute | solution.py:233
  24.3 21.5 %collective-permute-start.7 = (s32[2,24]{1,0:T(2,128)S(1)}, s32[2,24]{1,0:T(2,128)S(1)}, u32[]{:S(2)}, u32[]{:S(2)}) collective-permute-start(s32[2,24]{1,0:T(2,128)S(1)} %bitcast.88), channel_id=1, source_target_pairs={{32,0},{36,4},{40,8},{44,12},{48,16},{52,20},{56,24},{60,28},{0,32... | collective-permute-start | bytes 584 | tf_op jit(solution)/shard_map/ppermute | solution.py:233
  27.6 18.2 %collective-permute-start.8 = (s32[2,24]{1,0:T(2,128)S(1)}, s32[2,24]{1,0:T(2,128)S(1)}, u32[]{:S(2)}, u32[]{:S(2)}) collective-permute-start(s32[2,24]{1,0:T(2,128)S(1)} %bitcast.89), channel_id=1, source_target_pairs={{40,0},{44,4},{48,8},{52,12},{56,16},{60,20},{0,24},{4,28},{8,32},... | collective-permute-start | bytes 584 | tf_op jit(solution)/shard_map/ppermute | solution.py:233
  41.1 4.9 %collective-permute-start.9 = (s32[2,24]{1,0:T(2,128)S(1)}, s32[2,24]{1,0:T(2,128)S(1)}, u32[]{:S(2)}, u32[]{:S(2)}) collective-permute-start(s32[2,24]{1,0:T(2,128)S(1)} %bitcast.91), channel_id=1, source_target_pairs={{48,0},{52,4},{56,8},{60,12},{0,16},{4,20},{8,24},{12,28},{16,32},... | collective-permute-start | bytes 584 | tf_op jit(solution)/shard_map/ppermute | solution.py:233
  41.1 5.4 %collective-permute-start.10 = (s32[2,24]{1,0:T(2,128)S(1)}, s32[2,24]{1,0:T(2,128)S(1)}, u32[]{:S(2)}, u32[]{:S(2)}) collective-permute-start(s32[2,24]{1,0:T(2,128)S(1)} %bitcast.92), channel_id=1, source_target_pairs={{56,0},{60,4},{0,8},{4,12},{8,16},{12,20},{16,24},{20,28},{24,32},... | collective-permute-start | bytes 584 | tf_op jit(solution)/shard_map/ppermute | solution.py:233
  46.6 3.8 %collective-permute-start.11 = (s32[16,24]{1,0:T(8,128)S(1)}, s32[16,24]{1,0:T(8,128)S(1)}, u32[]{:S(2)}, u32[]{:S(2)}) collective-permute-start(s32[16,24]{1,0:T(8,128)S(1)} %bitcast.80), channel_id=1, source_target_pairs={{64,0},{68,4},{72,8},{76,12},{80,16},{84,20},{88,24},{92,28},{96,3... | collective-permute-start | bytes 4616 | tf_op jit(solution)/shard_map/ppermute | solution.py:233
  49.3 4.0 %collective-permute-start.12 = (s32[16,24]{1,0:T(8,128)S(1)}, s32[16,24]{1,0:T(8,128)S(1)}, u32[]{:S(2)}, u32[]{:S(2)}) collective-permute-start(s32[16,24]{1,0:T(8,128)S(1)} %bitcast.81), channel_id=1, source_target_pairs={{128,0},{132,4},{136,8},{140,12},{144,16},{148,20},{152,24},{156,2... | collective-permute-start | bytes 4616 | tf_op jit(solution)/shard_map/ppermute | solution.py:233
  49.6 3.7 %collective-permute-start.13 = (s32[16,24]{1,0:T(8,128)S(1)}, s32[16,24]{1,0:T(8,128)S(1)}, u32[]{:S(2)}, u32[]{:S(2)}) collective-permute-start(s32[16,24]{1,0:T(8,128)S(1)} %bitcast.82), channel_id=1, source_target_pairs={{192,0},{196,4},{200,8},{204,12},{208,16},{212,20},{216,24},{220,2... | collective-permute-start | bytes 4616 | tf_op jit(solution)/shard_map/ppermute | solution.py:233
  56.5 11.2 %copy-start = (bf16[1,12,32,128]{3,2,1,0:T(8,128)(2,1)S(1)}, bf16[1,12,32,128]{3,2,1,0:T(8,128)(2,1)}, u32[]{:S(2)}) copy-start(bf16[1,12,32,128]{3,2,1,0:T(8,128)(2,1)} %param.4) | copy-start | bytes 294916
  56.5 50.9 %all-to-all-start.1 = ((bf16[64,24,512]{2,1,0:T(8,128)(2,1)}), bf16[64,24,512]{2,1,0:T(8,128)(2,1)S(1)}, u32[]{:S(2)}, u32[]{:S(2)}) async-start(bf16[64,24,512]{2,1,0:T(8,128)(2,1)} %bitcast.20), calls=%async_computation.1 | async-start | bytes 3145728 | tf_op jit(solution)/shard_map/all_to_all | solution.py:22
  68.0 5.3 %collective-permute-start.2 = (bf16[384,128]{1,0:T(8,128)(2,1)S(1)}, bf16[384,128]{1,0:T(8,128)(2,1)S(1)}, u32[]{:S(2)}, u32[]{:S(2)}) collective-permute-start(bf16[384,128]{1,0:T(8,128)(2,1)S(1)} %fusion.8), channel_id=1, source_target_pairs={{3,0},{0,1},{1,2},{2,3},{7,4},{4,5},{5,6},{6,7},{11,8},{8,9},{9,10... | collective-permute-start | bytes 294920 | tf_op jit(solution)/shard_map/ppermute | solution.py:218
  69.4 7.2 %collective-permute-start.1 = (bf16[384,128]{1,0:T(8,128)(2,1)S(1)}, bf16[384,128]{1,0:T(8,128)(2,1)S(1)}, u32[]{:S(2)}, u32[]{:S(2)}) collective-permute-start(bf16[384,128]{1,0:T(8,128)(2,1)S(1)} %fusion.8), channel_id=1, source_target_pairs={{2,0},{3,1},{0,2},{1,3},{6,4},{7,5},{4,6},{5,7},{10,8},{11,9},{8,1... | collective-permute-start | bytes 294920 | tf_op jit(solution)/shard_map/ppermute | solution.py:218
  72.0 4.5 %collective-permute-start = (bf16[384,128]{1,0:T(8,128)(2,1)S(1)}, bf16[384,128]{1,0:T(8,128)(2,1)S(1)}, u32[]{:S(2)}, u32[]{:S(2)}) collective-permute-start(bf16[384,128]{1,0:T(8,128)(2,1)S(1)} %fusion.8), channel_id=1, source_target_pairs={{1,0},{2,1},{3,2},{0,3},{5,4},{6,5},{7,6},{4,7},{9,8},{10,9},{11,1... | collective-permute-start | bytes 294920 | tf_op jit(solution)/shard_map/ppermute | solution.py:218
  117.6 6.9 %collective-permute-start.16 = (f32[24,1536]{1,0:T(8,128)}, f32[24,1536]{1,0:T(8,128)S(1)}, u32[]{:S(2)}, u32[]{:S(2)}) collective-permute-start(f32[24,1536]{1,0:T(8,128)} %forward_totals.1), channel_id=1, source_target_pairs={{3,0},{0,1},{1,2},{2,3},{7,4},{4,5},{5,6},{6,7},{11,8},{8,9},{9,10... | collective-permute-start | bytes 442376 | tf_op jit(solution)/shard_map/ppermute | solution.py:218
  118.9 5.6 %collective-permute-start.14 = (f32[24,1536]{1,0:T(8,128)}, f32[24,1536]{1,0:T(8,128)S(1)}, u32[]{:S(2)}, u32[]{:S(2)}) collective-permute-start(f32[24,1536]{1,0:T(8,128)} %forward_totals.1), channel_id=1, source_target_pairs={{1,0},{2,1},{3,2},{0,3},{5,4},{6,5},{7,6},{4,7},{9,8},{10,9},{11,1... | collective-permute-start | bytes 442376 | tf_op jit(solution)/shard_map/ppermute | solution.py:218
  120.3 8.4 %collective-permute-start.15 = (f32[24,1536]{1,0:T(8,128)}, f32[24,1536]{1,0:T(8,128)S(1)}, u32[]{:S(2)}, u32[]{:S(2)}) collective-permute-start(f32[24,1536]{1,0:T(8,128)} %forward_totals.1), channel_id=1, source_target_pairs={{2,0},{3,1},{0,2},{1,3},{6,4},{7,5},{4,6},{5,7},{10,8},{11,9},{8,1... | collective-permute-start | bytes 442376 | tf_op jit(solution)/shard_map/ppermute | solution.py:218
  196.5 37.1 %all-to-all-start.3 = ((bf16[64,16,512]{2,1,0:T(8,128)(2,1)}), bf16[64,16,512]{2,1,0:T(8,128)(2,1)S(1)}, u32[]{:S(2)}, u32[]{:S(2)}) async-start(bf16[64,16,512]{2,1,0:T(8,128)(2,1)} %bitcast.27), calls=%async_computation.3 | async-start | bytes 2097152 | tf_op jit(solution)/shard_map/all_to_all | solution.py:22
  217.1 6.1 %collective-permute-start.19 = (f32[384,128]{1,0:T(8,128)S(1)}, f32[384,128]{1,0:T(8,128)S(1)}, u32[]{:S(2)}, u32[]{:S(2)}) collective-permute-start(f32[384,128]{1,0:T(8,128)S(1)} %get-tuple-element.8), channel_id=1, source_target_pairs={{1,0},{2,1},{3,2},{0,3},{5,4},{6,5},{7,6},{4,7},{9,8},{10,9},{11,1... | collective-permute-start | bytes 589832 | tf_op jit(solution)/shard_map/ppermute | solution.py:218
  218.9 7.3 %collective-permute-start.18 = (f32[384,128]{1,0:T(8,128)S(1)}, f32[384,128]{1,0:T(8,128)S(1)}, u32[]{:S(2)}, u32[]{:S(2)}) collective-permute-start(f32[384,128]{1,0:T(8,128)S(1)} %get-tuple-element.9), channel_id=1, source_target_pairs={{2,0},{3,1},{0,2},{1,3},{6,4},{7,5},{4,6},{5,7},{10,8},{11,9},{8,1... | collective-permute-start | bytes 589832 | tf_op jit(solution)/shard_map/ppermute | solution.py:218
  220.0 11.4 %collective-permute-start.17 = (f32[384,128]{1,0:T(8,128)S(1)}, f32[384,128]{1,0:T(8,128)S(1)}, u32[]{:S(2)}, u32[]{:S(2)}) collective-permute-start(f32[384,128]{1,0:T(8,128)S(1)} %get-tuple-element.7), channel_id=1, source_target_pairs={{3,0},{0,1},{1,2},{2,3},{7,4},{4,5},{5,6},{6,7},{11,8},{8,9},{9,10... | collective-permute-start | bytes 589832 | tf_op jit(solution)/shard_map/ppermute | solution.py:218

commit v3 on v2

v3 whole, which is shorter than its diff:
```python
import functools
import math

import jax
import jax.numpy as jnp
from jax import lax
from jax.experimental import pallas as pl
from jax.experimental.pallas import tpu as pltpu
from jax.sharding import PartitionSpec as P

SHARPNESS = 10.0
INV_TEMP = 20.0
LOSS_SCALE = 256.0
EPSILON = 1e-06
EXP2_SCALE = SHARPNESS * math.log2(math.e)
PER_STEP = 8
PER_LOOP = 4
GRAD_TYPE = jnp.bfloat16
OWN_TYPE = jnp.bfloat16


def exchange(value, axis):
    return lax.all_to_all(value, axis, split_axis=0, concat_axis=0, tiled=True)


def normalize(embeddings):
    values = embeddings.astype(jnp.float32)
    inverse = lax.rsqrt(jnp.sum(values * values, axis=-1, keepdims=True) + EPSILON)
    return (values * inverse, inverse)


def unnormalize_grad(unit_vectors, inverse, gradient):
    return inverse * (
        gradient - unit_vectors * jnp.sum(unit_vectors * gradient, axis=-1, keepdims=True)
    )


def coefficients(totals, tokens):
    candidates = totals.shape[0]
    queries_here = totals.shape[1] // tokens
    shaped = totals.reshape(candidates, queries_here, tokens)
    per_token = jnp.log(shaped) / SHARPNESS
    logits = INV_TEMP * jnp.mean(per_token, axis=2)
    exponentials = jnp.exp(logits)
    denominator = jnp.sum(exponentials, axis=0)
    losses = jnp.log(denominator) - logits[0]
    positive = (jnp.arange(candidates) == 0).astype(jnp.float32)[:, None]
    probability = exponentials / denominator
    scaled = LOSS_SCALE * INV_TEMP / tokens * (probability - positive)
    weights = scaled[:, :, None] / shaped
    return (weights.reshape(candidates, queries_here * tokens), losses)


def row_chunk(rows):
    return 256 if rows % 256 == 0 else rows


def load_pages(page_ref, raw_ref):
    pieces, per_step, _ = page_ref.shape
    depth, rows, width = raw_ref.shape
    for j in range(depth):
        block = page_ref[:, :, j * width : (j + 1) * width].astype(jnp.float32)
        raw_ref[j] = block.reshape(rows, width)


def candidate_rows(raw_ref, c, per_step):
    depth, rows, _ = raw_ref.shape
    parts = [raw_ref[j, pl.ds(c, rows // per_step, stride=per_step), :] for j in range(depth)]
    return jnp.concatenate(parts, axis=0)


def prepare(page_ref, raw_ref, unit_ref):
    per_step = page_ref.shape[1]
    load_pages(page_ref, raw_ref)
    patches = unit_ref.shape[0] // per_step
    for c in range(per_step):
        unit, _ = normalize(candidate_rows(raw_ref, c, per_step))
        unit_ref[c * patches : (c + 1) * patches, :] = unit.astype(jnp.bfloat16)
    return per_step, patches


def exponentials_of(unit_block, row_block):
    scores = lax.dot_general(
        unit_block, row_block, (((1,), (1,)), ((), ())), preferred_element_type=jnp.float32
    )
    return jnp.exp2(scores * EXP2_SCALE)


def patch_slice(c, patches):
    return pl.ds(pl.multiple_of(c * patches, patches), patches)


def forward_kernel(q_ref, page_ref, totals_ref, raw_ref, unit_ref):
    per_step, patches = prepare(page_ref, raw_ref, unit_ref)
    rows = q_ref.shape[0]
    chunk = row_chunk(rows)
    together = math.gcd(per_step, PER_LOOP)
    first = pl.program_id(0) * per_step

    @pl.loop(0, per_step // together)
    def _(turn):
        for start in range(0, rows, chunk):
            block = q_ref[start : start + chunk, :]
            for k in range(together):
                c = turn * together + k
                values = exponentials_of(unit_ref[patch_slice(c, patches), :], block)
                totals_ref[pl.ds(first + c, 1), start : start + chunk] = jnp.sum(
                    values, axis=0, keepdims=True
                )


def fill_shares(q_ref, weight_ref, unit_ref, share_ref, per_step, patches, turn):
    rows = q_ref.shape[0]
    chunk = row_chunk(rows)
    together = math.gcd(per_step, PER_LOOP)
    first = pl.program_id(0) * per_step
    for start in range(0, rows, chunk):
        block = q_ref[start : start + chunk, :]
        for k in range(together):
            c = turn * together + k
            values = exponentials_of(unit_ref[patch_slice(c, patches), :], block)
            weight = weight_ref[pl.ds(first + c, 1), start : start + chunk]
            share_ref[k * patches : (k + 1) * patches, start : start + chunk] = (
                weight * values
            ).astype(jnp.bfloat16)
    return together


def page_side_kernel(q_ref, page_ref, weight_ref, grad_ref, raw_ref, unit_ref, share_ref, back_ref):
    per_step, patches = prepare(page_ref, raw_ref, unit_ref)
    pieces = page_ref.shape[0]
    depth, _, width = raw_ref.shape

    @pl.loop(0, per_step // math.gcd(per_step, PER_LOOP))
    def _(turn):
        together = fill_shares(q_ref, weight_ref, unit_ref, share_ref, per_step, patches, turn)
        for k in range(together):
            back_ref[patch_slice(turn * together + k, patches), :] = jnp.dot(
                share_ref[k * patches : (k + 1) * patches, :],
                q_ref[...],
                preferred_element_type=jnp.float32,
            )

    for c in range(per_step):
        unit, inverse = normalize(candidate_rows(raw_ref, c, per_step))
        gradient = unnormalize_grad(unit, inverse, back_ref[c * patches : (c + 1) * patches, :])
        for j in range(depth):
            raw_ref[j, pl.ds(c, pieces, stride=per_step), :] = gradient[
                j * pieces : (j + 1) * pieces, :
            ]
    for j in range(depth):
        block = raw_ref[j].reshape(pieces, per_step, width)
        grad_ref[:, :, j * width : (j + 1) * width] = block.astype(grad_ref.dtype)


def query_side_kernel(
    q_ref, page_ref, weight_ref, rows_ref, raw_ref, unit_ref, share_ref, back_ref
):
    per_step, patches = prepare(page_ref, raw_ref, unit_ref)
    step = pl.program_id(0)

    @pl.when(step == 0)
    def _():
        back_ref[...] = jnp.zeros_like(back_ref)

    @pl.loop(0, per_step // math.gcd(per_step, PER_LOOP))
    def _(turn):
        together = fill_shares(q_ref, weight_ref, unit_ref, share_ref, per_step, patches, turn)
        back_ref[...] += lax.dot_general(
            unit_ref[patch_slice(turn, together * patches), :],
            share_ref[...],
            (((0,), (0,)), ((), ())),
            preferred_element_type=jnp.float32,
        )

    @pl.when(step == pl.num_programs(0) - 1)
    def _():
        rows_ref[...] = back_ref[...].T


def over_candidates(
    kernel, name, products, query_rows, fetched, weights, out_spec, out_shape, share, back
):
    rows, width = query_rows.shape
    pieces, candidates, wide = fetched.shape
    per_step = math.gcd(candidates, PER_STEP)
    patches = pieces * wide // width
    table = pl.BlockSpec((candidates, rows), lambda i: (0, 0))
    scratch = [
        pltpu.VMEM((wide // width, pieces * per_step, width), jnp.float32),
        pltpu.VMEM((per_step * patches, width), jnp.bfloat16),
    ]
    if share:
        together = math.gcd(per_step, PER_LOOP)
        scratch.append(pltpu.VMEM((together * patches, rows), jnp.bfloat16))
        scratch.append(pltpu.VMEM(back or (per_step * patches, width), jnp.float32))
    return pl.pallas_call(
        kernel,
        grid=(candidates // per_step,),
        in_specs=[
            pl.BlockSpec((rows, width), lambda i: (0, 0)),
            pl.BlockSpec((pieces, per_step, wide), lambda i: (0, i, 0)),
        ]
        + [table for _ in weights],
        out_specs=out_spec or table,
        out_shape=out_shape,
        scratch_shapes=scratch,
        cost_estimate=pl.CostEstimate(
            flops=2 * products * candidates * patches * rows * width,
            transcendentals=candidates * patches * rows,
            bytes_accessed=4 * candidates * patches * width,
        ),
        name=name,
    )(query_rows, fetched, *weights)


def forward_totals(query_rows, fetched):
    shape = jax.ShapeDtypeStruct((fetched.shape[1], query_rows.shape[0]), jnp.float32)
    return over_candidates(
        forward_kernel, "forward_totals", 1, query_rows, fetched, [], None, shape, False, None
    )


def page_side(query_rows, fetched, weights):
    pieces, candidates, wide = fetched.shape
    per_step = math.gcd(candidates, PER_STEP)
    spec = pl.BlockSpec((pieces, per_step, wide), lambda i: (0, i, 0))
    shape = jax.ShapeDtypeStruct(fetched.shape, GRAD_TYPE)
    return over_candidates(
        page_side_kernel, "page_side", 2, query_rows, fetched, [weights], spec, shape, True, None
    )


def query_side(query_rows, fetched, weights):
    spec = pl.BlockSpec(query_rows.shape, lambda i: (0, 0))
    shape = jax.ShapeDtypeStruct(query_rows.shape, jnp.float32)
    back = query_rows.shape[::-1]
    return over_candidates(
        query_side_kernel, "query_side", 2, query_rows, fetched, [weights], spec, shape, True, back
    )


def from_ahead(value, axis, shift):
    devices = lax.axis_size(axis)
    pairs = [((i + shift) % devices, i) for i in range(devices)]
    return lax.ppermute(value, axis, pairs)


ID_ROWS = 8


def local(queries, pages, cand_owner, cand_slot):
    queries_local, tokens, width = queries.shape[1:]
    local_pages, patches = pages.shape[:2]
    owners_count = lax.axis_size("pages")
    group = lax.axis_size("query")
    candidates = cand_owner.shape[1]
    rows_local = queries_local * tokens
    depth = patches // owners_count
    wide = depth * width
    pieces = pages.reshape(local_pages, depth, owners_count, width)
    spread = jnp.transpose(pieces, (2, 1, 0, 3)).reshape(owners_count, depth * local_pages, width)
    wanted = jnp.concatenate([cand_owner[0], cand_slot[0]]).astype(jnp.bfloat16)
    wanted = jnp.pad(wanted[None, :], ((0, ID_ROWS - 1), (0, width - 2 * candidates)))
    wanted = jnp.broadcast_to(wanted[None], (owners_count, ID_ROWS, width))
    arrived = exchange(jnp.concatenate([spread, wanted], axis=1), "pages")
    tiles = [arrived[:, j * local_pages : (j + 1) * local_pages, :] for j in range(depth)]
    table = jnp.concatenate(tiles, axis=2).reshape(owners_count * local_pages, wide)
    ids = arrived[:, depth * local_pages, : 2 * candidates].astype(jnp.int32)
    asked = ids[:, :candidates] * local_pages + ids[:, candidates:]
    asked = asked.reshape(owners_count * candidates)

    q_unit, q_inv = normalize(queries[0])
    q_round = q_unit.astype(jnp.bfloat16).reshape(rows_local, width)
    query_rows = jnp.concatenate(
        [q_round] + [from_ahead(q_round, "query", k) for k in range(1, group)], axis=0
    )

    page_range = jnp.arange(owners_count * local_pages, dtype=jnp.int32)
    picker = (asked[:, None] == page_range[None, :]).astype(jnp.bfloat16)
    served = jnp.dot(picker, table, preferred_element_type=jnp.float32).astype(jnp.bfloat16)
    fetched = exchange(served.reshape(owners_count, candidates, wide), "pages")

    partial_totals = forward_totals(query_rows, fetched)
    totals = partial_totals
    for k in range(1, group):
        theirs = from_ahead(partial_totals, "query", k)
        totals = totals + jnp.roll(theirs, k * rows_local, axis=1)
    weights, losses_all = coefficients(totals, tokens)
    losses = losses_all[:queries_local]

    returned = exchange(page_side(query_rows, fetched, weights), "pages")

    grad_rows = query_side(query_rows, fetched, weights).reshape(group, rows_local, width)
    own_grads = grad_rows[0]
    for k in range(1, group):
        own_grads = own_grads + from_ahead(grad_rows[k], "query", group - k)
    query_grad = unnormalize_grad(
        q_unit, q_inv, own_grads.reshape(queries_local, tokens, width)
    )
    returned, query_grad = lax.optimization_barrier((returned, query_grad))

    collector = (page_range[:, None] == asked[None, :]).astype(GRAD_TYPE)
    summed = jnp.dot(
        collector,
        returned.reshape(owners_count * candidates, wide),
        preferred_element_type=jnp.float32,
    )
    own = exchange(summed.astype(OWN_TYPE).reshape(owners_count, local_pages, wide), "pages")
    own = own.reshape(owners_count, local_pages, depth, width).astype(jnp.float32)
    page_grad = jnp.transpose(own, (1, 2, 0, 3)).reshape(pages.shape)
    return (losses[None, :], query_grad[None], page_grad)


def solution(mesh):
    return jax.shard_map(
        local,
        mesh=mesh,
        in_specs=(
            P("pages", "query", None, None),
            P("pages", "query", None),
            P("pages", None),
            P("pages", None),
        ),
        out_specs=(P("pages", "query"), P("pages", "query", None, None), P("pages", "query", None)),
        check_vma=False,
    )
```

time: 237 us -> 227 us (0.958)
  starting transfers between devices: 60.8 us -> 30.2 us
  waiting for transfers between devices: 69.2 us -> 91.4 us
  local copies, waits for them, and re-layouts: 13.1 us -> 9.08 us
  Pallas kernels: 35.9 us -> 39.6 us
    all_to_all x3, waiting for transfers between devices: 30.1 us -> 67.2 us  [exchange(): return lax.all_to_all(value, axis, split_axis=0, concat_axis=0, tiled=True)]
    ppermute x11 -> x0, starting transfers between devices: 18.1 us -> none  [gathered(): received.append(lax.ppermute(parts, axis, pairs))]
    ppermute x11 -> x0, waiting for transfers between devices: 18 us -> none  [gathered(): received.append(lax.ppermute(parts, axis, pairs))]
    all_to_all x3, starting transfers between devices: 30.4 us -> 19.2 us  [exchange(): return lax.all_to_all(value, axis, split_axis=0, concat_axis=0, tiled=True)]
    pallas_call x3, Pallas kernels: 35.9 us -> 39.6 us  [over_candidates(): pl.pallas_call(kernel, grid=(candidates // per_step,), in_specs=[pl.Block...]
    reshape x2 -> x0, local copies, waits for them, and re-layouts: 3.26 us -> none  [the longest x1 2.04 us: local(): pieces = pages.reshape(local_pages, depth, owners_count, width)]
    ppermute x9, waiting for transfers between devices: 21.1 us -> 24.2 us  [from_ahead(): return lax.ppermute(value, axis, pairs)]
  transfers between devices with their start and end apart: 23 -> 12, of which waited for: 14 -> 10; matrix products, arithmetic and copies ran while one was open for 2% -> 2% of each run, Pallas kernels for 6% -> 6%
where the time goes in v3:
time: 227 us
  waiting for transfers between devices  91.4 us (40%)
  blocking collectives  44.1 us (19%)
  Pallas kernels  39.6 us (17%)
  starting transfers between devices  30.2 us (13%)
  local copies, waits for them, and re-layouts  9.08 us (4%)
  matrix products  5.77 us (3%)
  other arithmetic  5.46 us (2%)
    all_to_all x3, waiting for transfers between devices, exchange(): return lax.all_to_all(value, axis, split_axis=0, concat_axis=0, tiled=True)  67.2 us
    all_to_all x1, blocking collectives, exchange(): return lax.all_to_all(value, axis, split_axis=0, concat_axis=0, tiled=True)  44.1 us
    pallas_call x3, Pallas kernels, over_candidates(): pl.pallas_call(kernel, grid=(candidates // per_step,), in_specs=[pl.Block...  39.6 us
    ppermute x9, waiting for transfers between devices, from_ahead(): return lax.ppermute(value, axis, pairs)  24.2 us
    all_to_all x3, starting transfers between devices, exchange(): return lax.all_to_all(value, axis, split_axis=0, concat_axis=0, tiled=True)  19.2 us
    ppermute x9, starting transfers between devices, from_ahead(): return lax.ppermute(value, axis, pairs)  11 us
  transfers between devices with their start and end apart: 12, of which 10 were waited for; matrix products, arithmetic and copies ran while one was open for 2% of the time, Pallas kernels for 6%

profile of v3, /device:TPU:1, one launch (start us, length us, event | category | flops | bytes accessed | tf_op | source)
XLA Modules:
  0.0 226.5 jit_solution(8954956911493213741)
XLA Ops:
  0.7 1.9 copy.9
  2.8 44.1 %all_to_all.20 = bf16[64,72,128]{2,1,0:T(8,128)(2,1)S(1)} all-to-all(bf16[64,72,128]{2,1,0:T(8,128)(2,1)S(1)} %pad_maximum_fusion), channel_id=1, replica_groups=mesh['pages'=64,'query'=4] {'pages'}, dimensions={0} | all-to-all | bytes 2359296 | tf_op jit(solution)/shard_map/all_to_all | solution.py:23
  47.5 3.0 %fusion.4 = bf16[1536,512]{1,0:T(8,128)(2,1)} fusion(bf16[1024,512]{1,0:T(8,128)(2,1)S(1)} %bitcast.43, s32[1536]{0:T(1024)S(1)} %eq.35), kind=kOutput, calls=%fused_computation.6 | convolution fusion | flops 1612972032 | bytes 2627584 | tf_op jit(solution)/shard_map/dot_general | solution.py:281
  50.5 6.3 %all-to-all-start.1 = ((bf16[64,24,512]{2,1,0:T(8,128)(2,1)}), bf16[64,24,512]{2,1,0:T(8,128)(2,1)S(1)}, u32[]{:S(2)}, u32[]{:S(2)}) async-start(bf16[64,24,512]{2,1,0:T(8,128)(2,1)} %bitcast.7), calls=%async_computation.1 | async-start | bytes 3145728 | tf_op jit(solution)/shard_map/all_to_all | solution.py:23
  57.1 2.8 %collective-permute-start = (bf16[384,128]{1,0:T(8,128)(2,1)S(1)}, bf16[384,128]{1,0:T(8,128)(2,1)S(1)}, u32[]{:S(2)}, u32[]{:S(2)}) collective-permute-start(bf16[384,128]{1,0:T(8,128)(2,1)S(1)} %fusion.12), channel_id=1, source_target_pairs={{1,0},{2,1},{3,2},{0,3},{5,4},{6,5},{7,6},{4,7},{9,8},{10,9},{11,1... | collective-permute-start | bytes 294920 | tf_op jit(solution)/shard_map/ppermute | solution.py:246
  60.3 0.7 collective-permute-start.2
  61.6 3.6 %collective-permute-done.1 = bf16[384,128]{1,0:T(8,128)(2,1)S(1)} collective-permute-done((bf16[384,128]{1,0:T(8,128)(2,1)S(1)}, bf16[384,128]{1,0:T(8,128)(2,1)S(1)}, u32[]{:S(2)}, u32[]{:S(2)}) %collective-permute-start.1) | collective-permute-done | bytes 98336 | tf_op jit(solution)/shard_map/ppermute | solution.py:246
  65.2 2.8 %collective-permute-done.2 = bf16[384,128]{1,0:T(8,128)(2,1)S(1)} collective-permute-done((bf16[384,128]{1,0:T(8,128)(2,1)S(1)}, bf16[384,128]{1,0:T(8,128)(2,1)S(1)}, u32[]{:S(2)}, u32[]{:S(2)}) %collective-permute-start.2) | collective-permute-done | bytes 98336 | tf_op jit(solution)/shard_map/ppermute | solution.py:246
  68.1 0.8 pad_maximum_fusion.2.q_ref
  68.8 27.7 %all-to-all-done.1.page_ref = bf16[64,24,512]{2,1,0:T(8,128)(2,1)S(1)} async-done(((bf16[64,24,512]{2,1,0:T(8,128)(2,1)}), bf16[64,24,512]{2,1,0:T(8,128)(2,1)S(1)}, u32[]{:S(2)}, u32[]{:S(2)}) %all-to-all-start.1) | async-done | bytes 1572896 | tf_op jit(solution)/shard_map/all_to_all | solution.py:23
  96.6 1.1 copy-done
  97.7 9.1 %forward_totals.1 = f32[24,1536]{1,0:T(8,128)} custom-call(bf16[1536,128]{1,0:T(8,128)(2,1)} %pad_maximum_fusion.2.q_ref, bf16[64,24,512]{2,1,0:T(8,128)(2,1)} %copy-done), custom_call_target="tpu_custom_call" | custom-call | flops 2415919104 | bytes 3145728 | tf_op jit(solution)/shard_map/forward_totals/pallas_call | solution.py:197
  106.8 2.7 %collective-permute-start.3 = (f32[24,1536]{1,0:T(8,128)}, f32[24,1536]{1,0:T(8,128)S(1)}, u32[]{:S(2)}, u32[]{:S(2)}) collective-permute-start(f32[24,1536]{1,0:T(8,128)} %forward_totals.1), channel_id=1, source_target_pairs={{1,0},{2,1},{3,2},{0,3},{5,4},{6,5},{7,6},{4,7},{9,8},{10,9},{11,1... | collective-permute-start | bytes 442376 | tf_op jit(solution)/shard_map/ppermute | solution.py:246
  109.5 1.6 collective-permute-start.4
  111.2 1.8 collective-permute-done.3
  113.0 6.2 %collective-permute-done.5 = f32[24,1536]{1,0:T(8,128)S(1)} collective-permute-done((f32[24,1536]{1,0:T(8,128)}, f32[24,1536]{1,0:T(8,128)S(1)}, u32[]{:S(2)}, u32[]{:S(2)}) %collective-permute-start.5) | collective-permute-done | bytes 147488 | tf_op jit(solution)/shard_map/ppermute | solution.py:246
  119.2 1.0 log_multiply_fusion
  121.2 0.7 div.40.weight_ref
  121.9 17.4 %page_side.1 = bf16[64,24,512]{2,1,0:T(8,128)(2,1)} custom-call(bf16[1536,128]{1,0:T(8,128)(2,1)} %pad_maximum_fusion.2.q_ref, bf16[64,24,512]{2,1,0:T(8,128)(2,1)} %copy-done, f32[24,1536]{1,0:T(8,128)} %div.40.weight_ref), custom_call_target="tpu_custom_call" | custom-call | flops 4831838208 | bytes 3145728 | tf_op jit(solution)/shard_map/page_side/pallas_call | solution.py:197
  139.3 6.8 %all-to-all-start.2 = ((bf16[64,24,512]{2,1,0:T(8,128)(2,1)}), bf16[64,24,512]{2,1,0:T(8,128)(2,1)S(1)}, u32[]{:S(2)}, u32[]{:S(2)}) async-start(bf16[64,24,512]{2,1,0:T(8,128)(2,1)} %page_side.1), calls=%async_computation.2 | async-start | bytes 3145728 | tf_op jit(solution)/shard_map/all_to_all | solution.py:23
  146.1 13.1 %query_side.1 = f32[1536,128]{1,0:T(8,128)} custom-call(bf16[1536,128]{1,0:T(8,128)(2,1)} %pad_maximum_fusion.2.q_ref, bf16[64,24,512]{2,1,0:T(8,128)(2,1)} %copy-done, f32[24,1536]{1,0:T(8,128)} %div.40.weight_ref), custom_call_target="tpu_custom_call" | custom-call | flops 4831838208 | bytes 3145728 | tf_op jit(solution)/shard_map/query_side/pallas_call | solution.py:197
  159.2 1.2 fusion.25
  160.5 1.0 collective-permute-start.7
  161.5 1.6 collective-permute-start.8
  163.1 8.7 %collective-permute-done.6 = f32[384,128]{1,0:T(8,128)S(1)} collective-permute-done((f32[384,128]{1,0:T(8,128)S(1)}, f32[384,128]{1,0:T(8,128)S(1)}, u32[]{:S(2)}, u32[]{:S(2)}) %collective-permute-start.6) | collective-permute-done | bytes 196640 | tf_op jit(solution)/shard_map/ppermute | solution.py:246
  172.3 1.2 multiply_reduce_fusion
  173.5 0.9 fusion.11
  174.4 11.5 %all-to-all-done.2 = bf16[64,24,512]{2,1,0:T(8,128)(2,1)S(1)} async-done(((bf16[64,24,512]{2,1,0:T(8,128)(2,1)}), bf16[64,24,512]{2,1,0:T(8,128)(2,1)S(1)}, u32[]{:S(2)}, u32[]{:S(2)}) %all-to-all-start.2) | async-done | bytes 1572896 | tf_op jit(solution)/shard_map/all_to_all | solution.py:23
  185.9 2.8 %fusion.5 = bf16[1024,512]{1,0:T(8,128)(2,1)} fusion(bf16[1536,512]{1,0:T(8,128)(2,1)S(1)} %bitcast.41, s32[1536]{0:T(1024)S(1)} %eq.35), kind=kOutput, calls=%fused_computation.7 | convolution fusion | flops 1612709888 | bytes 2627584 | tf_op jit(solution)/shard_map/dot_general | solution.py:304
  188.7 6.1 %all-to-all-start.3 = ((bf16[64,16,512]{2,1,0:T(8,128)(2,1)}), bf16[64,16,512]{2,1,0:T(8,128)(2,1)S(1)}, u32[]{:S(2)}, u32[]{:S(2)}) async-start(bf16[64,16,512]{2,1,0:T(8,128)(2,1)} %bitcast.13), calls=%async_computation.3 | async-start | bytes 2097152 | tf_op jit(solution)/shard_map/all_to_all | solution.py:23
  195.3 28.0 %all-to-all-done.3 = bf16[64,16,512]{2,1,0:T(8,128)(2,1)S(1)} async-done(((bf16[64,16,512]{2,1,0:T(8,128)(2,1)}), bf16[64,16,512]{2,1,0:T(8,128)(2,1)S(1)}, u32[]{:S(2)}, u32[]{:S(2)}) %all-to-all-start.3) | async-done | bytes 1048608 | tf_op jit(solution)/shard_map/all_to_all | solution.py:23
  224.0 2.5 %copy.10 = f32[64,16,4,128]{3,0,2,1:T(8,128)} copy(f32[64,16,4,128]{3,2,1,0:T(4,128)S(1)} %reshape.158) | data formatting | bytes 4194304 | tf_op jit(solution)/shard_map/reshape | solution.py:311
  (44 shorter events, 4.8 us)
Async XLA Ops:
  0.6 1.9 copy-start.2
  0.6 2.0 copy-start.3
  50.5 6.3 %copy-start.1 = (bf16[1,12,32,128]{3,2,1,0:T(8,128)(2,1)S(1)}, bf16[1,12,32,128]{3,2,1,0:T(8,128)(2,1)}, u32[]{:S(2)}) copy-start(bf16[1,12,32,128]{3,2,1,0:T(8,128)(2,1)} %param.4) | copy-start | bytes 294916
  50.5 46.1 %all-to-all-start.1 = ((bf16[64,24,512]{2,1,0:T(8,128)(2,1)}), bf16[64,24,512]{2,1,0:T(8,128)(2,1)S(1)}, u32[]{:S(2)}, u32[]{:S(2)}) async-start(bf16[64,24,512]{2,1,0:T(8,128)(2,1)} %bitcast.7), calls=%async_computation.1 | async-start | bytes 3145728 | tf_op jit(solution)/shard_map/all_to_all | solution.py:23
  57.1 4.4 %collective-permute-start = (bf16[384,128]{1,0:T(8,128)(2,1)S(1)}, bf16[384,128]{1,0:T(8,128)(2,1)S(1)}, u32[]{:S(2)}, u32[]{:S(2)}) collective-permute-start(bf16[384,128]{1,0:T(8,128)(2,1)S(1)} %fusion.12), channel_id=1, source_target_pairs={{1,0},{2,1},{3,2},{0,3},{5,4},{6,5},{7,6},{4,7},{9,8},{10,9},{11,1... | collective-permute-start | bytes 294920 | tf_op jit(solution)/shard_map/ppermute | solution.py:246
  59.9 5.3 %collective-permute-start.1 = (bf16[384,128]{1,0:T(8,128)(2,1)S(1)}, bf16[384,128]{1,0:T(8,128)(2,1)S(1)}, u32[]{:S(2)}, u32[]{:S(2)}) collective-permute-start(bf16[384,128]{1,0:T(8,128)(2,1)S(1)} %fusion.12), channel_id=1, source_target_pairs={{2,0},{3,1},{0,2},{1,3},{6,4},{7,5},{4,6},{5,7},{10,8},{11,9},{8,1... | collective-permute-start | bytes 294920 | tf_op jit(solution)/shard_map/ppermute | solution.py:246
  60.3 7.8 %collective-permute-start.2 = (bf16[384,128]{1,0:T(8,128)(2,1)S(1)}, bf16[384,128]{1,0:T(8,128)(2,1)S(1)}, u32[]{:S(2)}, u32[]{:S(2)}) collective-permute-start(bf16[384,128]{1,0:T(8,128)(2,1)S(1)} %fusion.12), channel_id=1, source_target_pairs={{3,0},{0,1},{1,2},{2,3},{7,4},{4,5},{5,6},{6,7},{11,8},{8,9},{9,10... | collective-permute-start | bytes 294920 | tf_op jit(solution)/shard_map/ppermute | solution.py:246
  96.6 1.1 copy-start
  106.8 6.2 %collective-permute-start.3 = (f32[24,1536]{1,0:T(8,128)}, f32[24,1536]{1,0:T(8,128)S(1)}, u32[]{:S(2)}, u32[]{:S(2)}) collective-permute-start(f32[24,1536]{1,0:T(8,128)} %forward_totals.1), channel_id=1, source_target_pairs={{1,0},{2,1},{3,2},{0,3},{5,4},{6,5},{7,6},{4,7},{9,8},{10,9},{11,1... | collective-permute-start | bytes 442376 | tf_op jit(solution)/shard_map/ppermute | solution.py:246
  109.5 9.7 %collective-permute-start.5 = (f32[24,1536]{1,0:T(8,128)}, f32[24,1536]{1,0:T(8,128)S(1)}, u32[]{:S(2)}, u32[]{:S(2)}) collective-permute-start(f32[24,1536]{1,0:T(8,128)} %forward_totals.1), channel_id=1, source_target_pairs={{3,0},{0,1},{1,2},{2,3},{7,4},{4,5},{5,6},{6,7},{11,8},{8,9},{9,10... | collective-permute-start | bytes 442376 | tf_op jit(solution)/shard_map/ppermute | solution.py:246
  109.5 9.7 %collective-permute-start.4 = (f32[24,1536]{1,0:T(8,128)}, f32[24,1536]{1,0:T(8,128)S(1)}, u32[]{:S(2)}, u32[]{:S(2)}) collective-permute-start(f32[24,1536]{1,0:T(8,128)} %forward_totals.1), channel_id=1, source_target_pairs={{2,0},{3,1},{0,2},{1,3},{6,4},{7,5},{4,6},{5,7},{10,8},{11,9},{8,1... | collective-permute-start | bytes 442376 | tf_op jit(solution)/shard_map/ppermute | solution.py:246
  139.3 46.6 %all-to-all-start.2 = ((bf16[64,24,512]{2,1,0:T(8,128)(2,1)}), bf16[64,24,512]{2,1,0:T(8,128)(2,1)S(1)}, u32[]{:S(2)}, u32[]{:S(2)}) async-start(bf16[64,24,512]{2,1,0:T(8,128)(2,1)} %page_side.1), calls=%async_computation.2 | async-start | bytes 3145728 | tf_op jit(solution)/shard_map/all_to_all | solution.py:23
  160.4 11.5 %collective-permute-start.6 = (f32[384,128]{1,0:T(8,128)S(1)}, f32[384,128]{1,0:T(8,128)S(1)}, u32[]{:S(2)}, u32[]{:S(2)}) collective-permute-start(f32[384,128]{1,0:T(8,128)S(1)} %get-tuple-element.15), channel_id=1, source_target_pairs={{3,0},{0,1},{1,2},{2,3},{7,4},{4,5},{5,6},{6,7},{11,8},{8,9},{9,10... | collective-permute-start | bytes 589832 | tf_op jit(solution)/shard_map/ppermute | solution.py:246
  160.5 11.4 %collective-permute-start.7 = (f32[384,128]{1,0:T(8,128)S(1)}, f32[384,128]{1,0:T(8,128)S(1)}, u32[]{:S(2)}, u32[]{:S(2)}) collective-permute-start(f32[384,128]{1,0:T(8,128)S(1)} %get-tuple-element.17), channel_id=1, source_target_pairs={{2,0},{3,1},{0,2},{1,3},{6,4},{7,5},{4,6},{5,7},{10,8},{11,9},{8,1... | collective-permute-start | bytes 589832 | tf_op jit(solution)/shard_map/ppermute | solution.py:246
  161.5 10.8 %collective-permute-start.8 = (f32[384,128]{1,0:T(8,128)S(1)}, f32[384,128]{1,0:T(8,128)S(1)}, u32[]{:S(2)}, u32[]{:S(2)}) collective-permute-start(f32[384,128]{1,0:T(8,128)S(1)} %get-tuple-element.16), channel_id=1, source_target_pairs={{1,0},{2,1},{3,2},{0,3},{5,4},{6,5},{7,6},{4,7},{9,8},{10,9},{11,1... | collective-permute-start | bytes 589832 | tf_op jit(solution)/shard_map/ppermute | solution.py:246
  188.7 34.6 %all-to-all-start.3 = ((bf16[64,16,512]{2,1,0:T(8,128)(2,1)}), bf16[64,16,512]{2,1,0:T(8,128)(2,1)S(1)}, u32[]{:S(2)}, u32[]{:S(2)}) async-start(bf16[64,16,512]{2,1,0:T(8,128)(2,1)} %bitcast.13), calls=%async_computation.3 | async-start | bytes 2097152 | tf_op jit(solution)/shard_map/all_to_all | solution.py:23

commit v4 on v3

v4 whole, which is shorter than its diff:
```python
import functools
import math

import jax
import jax.numpy as jnp
from jax import lax
from jax.experimental import pallas as pl
from jax.experimental.pallas import tpu as pltpu
from jax.sharding import PartitionSpec as P

SHARPNESS = 10.0
INV_TEMP = 20.0
LOSS_SCALE = 256.0
EPSILON = 1e-06
EXP2_SCALE = SHARPNESS * math.log2(math.e)
PER_STEP = 8
PER_LOOP = 4
FIRST_CHUNK = 8
PARAMS = pltpu.CompilerParams(vmem_limit_bytes=24 << 20)
GRAD_TYPE = jnp.bfloat16
OWN_TYPE = jnp.bfloat16


def exchange(value, axis):
    return lax.all_to_all(value, axis, split_axis=0, concat_axis=0, tiled=True)


def normalize(embeddings):
    values = embeddings.astype(jnp.float32)
    inverse = lax.rsqrt(jnp.sum(values * values, axis=-1, keepdims=True) + EPSILON)
    return (values * inverse, inverse)


def unnormalize_grad(unit_vectors, inverse, gradient):
    return inverse * (
        gradient - unit_vectors * jnp.sum(unit_vectors * gradient, axis=-1, keepdims=True)
    )


def group_sums(values, size):
    lanes = values.shape[1]
    lane = lax.broadcasted_iota(jnp.int32, values.shape, 1)
    step = 1
    while step < size:
        ahead = pltpu.roll(values, lanes - step, 1)
        behind = pltpu.roll(values, step, 1)
        values = values + jnp.where((lane // step) % 2 == 0, ahead, behind)
        step *= 2
    return values


def weights_kernel(tokens, shifts, *refs):
    weight_ref, loss_ref = refs[-2:]
    rows = weight_ref.shape[1]
    group = len(shifts)
    tile = math.gcd(rows // group, 128)
    for start in range(0, rows, tile):
        totals = []
        for first in range(0, len(refs) - 2, group):
            total = None
            for ref, shift in zip(refs[first : first + group], shifts):
                at = (start - shift) % rows
                part = ref[:, at : at + tile]
                total = part if total is None else total + part
            totals.append(total)
        totals = jnp.concatenate(totals, axis=0)
        per_token = jnp.log(totals) / SHARPNESS
        logits = INV_TEMP * (group_sums(per_token, tokens) / tokens)
        exponentials = jnp.exp(logits)
        denominator = jnp.sum(exponentials, axis=0, keepdims=True)
        loss_ref[:, start : start + tile] = jnp.log(denominator) - logits[:1]
        candidate = lax.broadcasted_iota(jnp.int32, totals.shape, 0)
        positive = jnp.where(candidate == 0, 1.0, 0.0)
        scaled = LOSS_SCALE * INV_TEMP / tokens * (exponentials / denominator - positive)
        weight_ref[:, start : start + tile] = scaled / totals


def weights_of(chunks, shifts, tokens):
    rows = chunks[0][0].shape[1]
    candidates = sum(parts[0].shape[0] for parts in chunks)
    return pl.pallas_call(
        functools.partial(weights_kernel, tokens, shifts),
        out_shape=[
            jax.ShapeDtypeStruct((candidates, rows), jnp.float32),
            jax.ShapeDtypeStruct((1, rows), jnp.float32),
        ],
        compiler_params=PARAMS,
        name="weights",
    )(*[part for parts in chunks for part in parts])


def row_chunk(rows):
    return 256 if rows % 256 == 0 else rows


def load_pages(page_ref, raw_ref):
    pieces, per_step, _ = page_ref.shape
    depth, rows, width = raw_ref.shape
    for j in range(depth):
        block = page_ref[:, :, j * width : (j + 1) * width].astype(jnp.float32)
        raw_ref[j] = block.reshape(rows, width)


def candidate_rows(raw_ref, c, per_step):
    depth, rows, _ = raw_ref.shape
    parts = [raw_ref[j, pl.ds(c, rows // per_step, stride=per_step), :] for j in range(depth)]
    return jnp.concatenate(parts, axis=0)


def prepare(raw_ref, unit_ref, k, c, per_step):
    unit, inverse = normalize(candidate_rows(raw_ref, c, per_step))
    patches = unit.shape[0]
    unit_ref[k * patches : (k + 1) * patches, :] = unit.astype(jnp.bfloat16)
    return unit, inverse


def exponentials_of(unit_block, row_block):
    scores = lax.dot_general(
        unit_block, row_block, (((1,), (1,)), ((), ())), preferred_element_type=jnp.float32
    )
    return jnp.exp2(scores * EXP2_SCALE)


def fill(q_ref, raw_ref, unit_ref, turn, per_step, use):
    rows = q_ref.shape[0]
    chunk = row_chunk(rows)
    together = math.gcd(per_step, PER_LOOP)
    patches = unit_ref.shape[0] // together
    first = turn * together
    for k in range(together):
        prepare(raw_ref, unit_ref, k, first + k, per_step)
    for start in range(0, rows, chunk):
        block = q_ref[start : start + chunk, :]
        for k in range(together):
            values = exponentials_of(unit_ref[k * patches : (k + 1) * patches, :], block)
            use(k, patches, pl.ds(start, chunk), values)
    return together, patches, first


def share_into(share_ref, weight_ref, row):
    def use(k, patches, columns, values):
        share = weight_ref[pl.ds(row + k, 1), columns] * values
        share_ref[k * patches : (k + 1) * patches, columns] = share.astype(jnp.bfloat16)

    return use


def forward_kernel(q_ref, page_ref, totals_ref, raw_ref, unit_ref):
    per_step = page_ref.shape[1]
    load_pages(page_ref, raw_ref)
    step_first = pl.program_id(0) * per_step
    together = math.gcd(per_step, PER_LOOP)

    @pl.loop(0, per_step // together)
    def _(turn):
        def use(k, patches, columns, values):
            row = pl.ds(step_first + turn * together + k, 1)
            totals_ref[row, columns] = jnp.sum(values, axis=0, keepdims=True)

        fill(q_ref, raw_ref, unit_ref, turn, per_step, use)


def page_side_kernel(offset, q_ref, page_ref, weight_ref, grad_ref, raw_ref, unit_ref, share_ref):
    per_step = page_ref.shape[1]
    pieces = page_ref.shape[0]
    depth, _, width = raw_ref.shape
    load_pages(page_ref, raw_ref)
    step_first = offset + pl.program_id(0) * per_step

    @pl.loop(0, per_step // math.gcd(per_step, PER_LOOP))
    def _(turn):
        use = share_into(share_ref, weight_ref, step_first + turn * math.gcd(per_step, PER_LOOP))
        together, patches, first = fill(q_ref, raw_ref, unit_ref, turn, per_step, use)
        for k in range(together):
            gradient = jnp.dot(
                share_ref[k * patches : (k + 1) * patches, :],
                q_ref[...],
                preferred_element_type=jnp.float32,
            )
            unit, inverse = normalize(candidate_rows(raw_ref, first + k, per_step))
            gradient = unnormalize_grad(unit, inverse, gradient)
            for j in range(depth):
                raw_ref[j, pl.ds(first + k, pieces, stride=per_step), :] = gradient[
                    j * pieces : (j + 1) * pieces, :
                ]

    for j in range(depth):
        block = raw_ref[j].reshape(pieces, per_step, width)
        grad_ref[:, :, j * width : (j + 1) * width] = block.astype(grad_ref.dtype)


def query_side_kernel(
    q_ref, page_ref, weight_ref, rows_ref, raw_ref, unit_ref, share_ref, back_ref
):
    per_step = page_ref.shape[1]
    load_pages(page_ref, raw_ref)
    step = pl.program_id(0)
    step_first = step * per_step

    @pl.when(step == 0)
    def _():
        back_ref[...] = jnp.zeros_like(back_ref)

    @pl.loop(0, per_step // math.gcd(per_step, PER_LOOP))
    def _(turn):
        use = share_into(share_ref, weight_ref, step_first + turn * math.gcd(per_step, PER_LOOP))
        fill(q_ref, raw_ref, unit_ref, turn, per_step, use)
        back_ref[...] += lax.dot_general(
            unit_ref[...],
            share_ref[...],
            (((0,), (0,)), ((), ())),
            preferred_element_type=jnp.float32,
        )

    @pl.when(step == pl.num_programs(0) - 1)
    def _():
        rows_ref[...] = back_ref[...].T


def output_kernel(page_ref, out_ref, raw_ref):
    load_pages(page_ref, raw_ref)
    for c in range(page_ref.shape[1]):
        out_ref[c] = candidate_rows(raw_ref, c, page_ref.shape[1])


def in_page_order(own, width):
    pieces, pages, wide = own.shape
    per_step = math.gcd(pages, PER_STEP)
    patches = pieces * wide // width
    return pl.pallas_call(
        output_kernel,
        grid=(pages // per_step,),
        in_specs=[pl.BlockSpec((pieces, per_step, wide), lambda i: (0, i, 0))],
        out_specs=pl.BlockSpec((per_step, patches, width), lambda i: (i, 0, 0)),
        out_shape=jax.ShapeDtypeStruct((pages, patches, width), jnp.float32),
        scratch_shapes=[pltpu.VMEM((wide // width, pieces * per_step, width), jnp.float32)],
        compiler_params=PARAMS,
        name="page_order",
    )(own)


def over_candidates(
    kernel, name, products, query_rows, fetched, weights, out_spec, out_shape, back, window=None
):
    rows, width = query_rows.shape
    pieces, candidates, wide = fetched.shape
    per_step = math.gcd(candidates, PER_STEP)
    first_step = 0
    if window:
        per_step = math.gcd(*window, per_step)
        first_step, candidates = window[0] // per_step, window[1]
    together = math.gcd(per_step, PER_LOOP)
    patches = pieces * wide // width
    scratch = [
        pltpu.VMEM((wide // width, pieces * per_step, width), jnp.float32),
        pltpu.VMEM((together * patches, width), jnp.bfloat16),
    ]
    if weights:
        scratch.append(pltpu.VMEM((together * patches, rows), jnp.bfloat16))
    if back:
        scratch.append(pltpu.VMEM((width, rows), jnp.float32))
    return pl.pallas_call(
        kernel,
        grid=(candidates // per_step,),
        in_specs=[
            pl.BlockSpec((rows, width), lambda i: (0, 0)),
            pl.BlockSpec((pieces, per_step, wide), lambda i: (0, i + first_step, 0)),
        ]
        + [pl.BlockSpec(table.shape, lambda i: (0, 0)) for table in weights],
        out_specs=out_spec,
        out_shape=out_shape,
        scratch_shapes=scratch,
        cost_estimate=pl.CostEstimate(
            flops=2 * products * candidates * patches * rows * width,
            transcendentals=candidates * patches * rows,
            bytes_accessed=4 * candidates * patches * width,
        ),
        compiler_params=PARAMS,
        name=name,
    )(query_rows, fetched, *weights)


def forward_totals(query_rows, fetched):
    shape = jax.ShapeDtypeStruct((fetched.shape[1], query_rows.shape[0]), jnp.float32)
    spec = pl.BlockSpec(shape.shape, lambda i: (0, 0))
    return over_candidates(
        forward_kernel, "forward_totals", 1, query_rows, fetched, [], spec, shape, False
    )


def page_side(query_rows, fetched, weights, window):
    pieces, candidates, wide = fetched.shape
    per_step = math.gcd(*window, candidates, PER_STEP)
    spec = pl.BlockSpec((pieces, per_step, wide), lambda i: (0, i, 0))
    shape = jax.ShapeDtypeStruct((pieces, window[1], wide), GRAD_TYPE)
    kernel = functools.partial(page_side_kernel, window[0])
    return over_candidates(
        kernel, "page_side", 2, query_rows, fetched, [weights], spec, shape, False, window
    )


def query_side(query_rows, fetched, weights):
    spec = pl.BlockSpec(query_rows.shape, lambda i: (0, 0))
    shape = jax.ShapeDtypeStruct(query_rows.shape, jnp.float32)
    return over_candidates(
        query_side_kernel, "query_side", 2, query_rows, fetched, [weights], spec, shape, True
    )


def from_ahead(value, axis, shift):
    devices = lax.axis_size(axis)
    pairs = [((i + shift) % devices, i) for i in range(devices)]
    return lax.ppermute(value, axis, pairs)


ID_ROWS = 8


def local(queries, pages, cand_owner, cand_slot):
    queries_local, tokens, width = queries.shape[1:]
    local_pages, patches = pages.shape[:2]
    owners_count = lax.axis_size("pages")
    group = lax.axis_size("query")
    candidates = cand_owner.shape[1]
    rows_local = queries_local * tokens
    depth = patches // owners_count
    wide = depth * width
    pieces = pages.reshape(local_pages, depth, owners_count, width)
    spread = jnp.transpose(pieces, (2, 1, 0, 3)).reshape(owners_count, depth * local_pages, width)
    wanted = jnp.concatenate([cand_owner[0], cand_slot[0]]).astype(jnp.bfloat16)
    wanted = jnp.pad(wanted[None, :], ((0, ID_ROWS - 1), (0, width - 2 * candidates)))
    wanted = jnp.broadcast_to(wanted[None], (owners_count, ID_ROWS, width))
    arrived = exchange(jnp.concatenate([spread, wanted], axis=1), "pages")
    tiles = [arrived[:, j * local_pages : (j + 1) * local_pages, :] for j in range(depth)]
    table = jnp.concatenate(tiles, axis=2).reshape(owners_count * local_pages, wide)
    ids = arrived[:, depth * local_pages, : 2 * candidates].astype(jnp.int32)
    asked = ids[:, :candidates] * local_pages + ids[:, candidates:]

    q_unit, q_inv = normalize(queries[0])
    q_round = q_unit.astype(jnp.bfloat16).reshape(rows_local, width)
    query_rows = jnp.concatenate(
        [q_round] + [from_ahead(q_round, "query", k) for k in range(1, group)], axis=0
    )

    page_range = jnp.arange(owners_count * local_pages, dtype=jnp.int32)
    picker = (asked.reshape(-1)[:, None] == page_range[None, :]).astype(jnp.bfloat16)
    served = jnp.dot(picker, table, preferred_element_type=jnp.float32).astype(jnp.bfloat16)
    fetched = exchange(served.reshape(owners_count, candidates, wide), "pages")

    own = forward_totals(query_rows, fetched)
    totals = [own] + [from_ahead(own, "query", k) for k in range(1, group)]
    weights, row_losses = weights_of([totals], [k * rows_local for k in range(group)], tokens)
    losses = row_losses[0, :rows_local].reshape(queries_local, tokens)[:, 0]

    edge = FIRST_CHUNK if candidates > FIRST_CHUNK else candidates // 2
    windows = ((0, edge), (edge, candidates - edge))
    terms = [page_side(query_rows, fetched, weights, windows[0])]
    terms.append(page_side(query_rows, fetched, weights, windows[1]))
    returned = [exchange(part, "pages") for part in terms]
    returned[0], weights = lax.optimization_barrier((returned[0], weights))

    grad_rows = query_side(query_rows, fetched, weights).reshape(group, rows_local, width)
    own_grads = grad_rows[0]
    for k in range(1, group):
        own_grads = own_grads + from_ahead(grad_rows[k], "query", group - k)
    query_grad = unnormalize_grad(
        q_unit, q_inv, own_grads.reshape(queries_local, tokens, width)
    )
    returned[1], query_grad = lax.optimization_barrier((returned[1], query_grad))

    summed = 0.0
    for part, (low, count) in zip(returned, windows):
        rows = asked[:, low : low + count].reshape(-1)
        collector = (page_range[:, None] == rows[None, :]).astype(GRAD_TYPE)
        summed = summed + jnp.dot(
            collector, part.reshape(-1, wide), preferred_element_type=jnp.float32
        )
    own = exchange(summed.astype(OWN_TYPE).reshape(owners_count, local_pages, wide), "pages")
    page_grad = in_page_order(own, width)
    return (losses[None, :], query_grad[None], page_grad)


def solution(mesh):
    return jax.shard_map(
        local,
        mesh=mesh,
        in_specs=(
            P("pages", "query", None, None),
            P("pages", "query", None),
            P("pages", None),
            P("pages", None),
        ),
        out_specs=(P("pages", "query"), P("pages", "query", None, None), P("pages", "query", None)),
        check_vma=False,
    )
```

time: 227 us -> 225 us (level)
  starting transfers between devices: 30.2 us -> 37.1 us
  local copies, waits for them, and re-layouts: 9.08 us -> 4.18 us
  Pallas kernels: 39.6 us -> 35.8 us
  other arithmetic: 5.46 us -> 1.78 us
    all_to_all x3 -> x4, starting transfers between devices: 19.2 us -> 26.7 us  [exchange(): return lax.all_to_all(value, axis, split_axis=0, concat_axis=0, tiled=True)]
    pallas_call x3 -> x4, Pallas kernels: 39.6 us -> 33.5 us  [over_candidates(): pl.pallas_call(kernel, grid=(candidates // per_step,), in_specs=[pl.Block...]
    reshape x2 -> x0, local copies, waits for them, and re-layouts: 3.21 us -> none  [local(): page_grad = jnp.transpose(own, (1, 2, 0, 3)).reshape(pages.shape)]
    all_to_all x3 -> x4, waiting for transfers between devices: 67.2 us -> 67.6 us  [exchange(): return lax.all_to_all(value, axis, split_axis=0, concat_axis=0, tiled=True)]
  transfers between devices with their start and end apart: 12 -> 13, of which waited for: 10 -> 12; matrix products, arithmetic and copies ran while one was open for 2% -> 1% of each run, Pallas kernels for 6% -> 10%
where the time goes in v4:
time: 225 us; the launch traced here: 224 us
  waiting for transfers between devices  93 us (41%)
  blocking collectives  44.1 us (20%)
  starting transfers between devices  37.1 us (16%)
  Pallas kernels  35.8 us (16%)
  matrix products  7.22 us (3%)
  local copies, waits for them, and re-layouts  4.18 us (2%)
    all_to_all x4, waiting for transfers between devices, exchange(): return lax.all_to_all(value, axis, split_axis=0, concat_axis=0, tiled=True)  67.6 us
    all_to_all x1, blocking collectives, exchange(): return lax.all_to_all(value, axis, split_axis=0, concat_axis=0, tiled=True)  44.1 us
    pallas_call x4, Pallas kernels, over_candidates(): pl.pallas_call(kernel, grid=(candidates // per_step,), in_specs=[pl.Block...  33.5 us
    all_to_all x4, starting transfers between devices, exchange(): return lax.all_to_all(value, axis, split_axis=0, concat_axis=0, tiled=True)  26.7 us
    ppermute x9, waiting for transfers between devices, from_ahead(): return lax.ppermute(value, axis, pairs)  25.4 us
    ppermute x9, starting transfers between devices, from_ahead(): return lax.ppermute(value, axis, pairs)  10.4 us
  transfers between devices with their start and end apart: 13, of which 12 were waited for; matrix products, arithmetic and copies ran while one was open for 1% of the time, Pallas kernels for 10%

profile of v4, /device:TPU:1, one launch (start us, length us, event | category | flops | bytes accessed | tf_op | source)
XLA Modules:
  0.0 224.0 jit_solution(5698103165574195525)
XLA Ops:
  0.7 1.9 copy.9
  2.8 44.1 %all_to_all.25 = bf16[64,72,128]{2,1,0:T(8,128)(2,1)S(1)} all-to-all(bf16[64,72,128]{2,1,0:T(8,128)(2,1)S(1)} %pad_maximum_fusion), channel_id=1, replica_groups=mesh['pages'=64,'query'=4] {'pages'}, dimensions={0} | all-to-all | bytes 2359296 | tf_op jit(solution)/shard_map/all_to_all | solution.py:25
  47.5 3.0 %fusion.3 = bf16[1536,512]{1,0:T(8,128)(2,1)} fusion(bf16[1024,512]{1,0:T(8,128)(2,1)S(1)} %bitcast.38, s32[1536]{0:T(1024)S(1)} %eq.45), kind=kOutput, calls=%fused_computation.5 | convolution fusion | flops 1612972032 | bytes 2627584 | tf_op jit(solution)/shard_map/dot_general | solution.py:347
  50.5 6.3 %all-to-all-start.1 = ((bf16[64,24,512]{2,1,0:T(8,128)(2,1)}), bf16[64,24,512]{2,1,0:T(8,128)(2,1)S(1)}, u32[]{:S(2)}, u32[]{:S(2)}) async-start(bf16[64,24,512]{2,1,0:T(8,128)(2,1)} %bitcast.7), calls=%async_computation.1 | async-start | bytes 3145728 | tf_op jit(solution)/shard_map/all_to_all | solution.py:25
  57.1 2.8 %collective-permute-start = (bf16[384,128]{1,0:T(8,128)(2,1)S(1)}, bf16[384,128]{1,0:T(8,128)(2,1)S(1)}, u32[]{:S(2)}, u32[]{:S(2)}) collective-permute-start(bf16[384,128]{1,0:T(8,128)(2,1)S(1)} %fusion.14), channel_id=1, source_target_pairs={{1,0},{2,1},{3,2},{0,3},{5,4},{6,5},{7,6},{4,7},{9,8},{10,9},{11,1... | collective-permute-start | bytes 294920 | tf_op jit(solution)/shard_map/ppermute | solution.py:313
  60.3 0.7 collective-permute-start.2
  61.6 3.6 %collective-permute-done.1 = bf16[384,128]{1,0:T(8,128)(2,1)S(1)} collective-permute-done((bf16[384,128]{1,0:T(8,128)(2,1)S(1)}, bf16[384,128]{1,0:T(8,128)(2,1)S(1)}, u32[]{:S(2)}, u32[]{:S(2)}) %collective-permute-start.1) | collective-permute-done | bytes 98336 | tf_op jit(solution)/shard_map/ppermute | solution.py:313
  65.2 2.8 %collective-permute-done.2 = bf16[384,128]{1,0:T(8,128)(2,1)S(1)} collective-permute-done((bf16[384,128]{1,0:T(8,128)(2,1)S(1)}, bf16[384,128]{1,0:T(8,128)(2,1)S(1)}, u32[]{:S(2)}, u32[]{:S(2)}) %collective-permute-start.2) | collective-permute-done | bytes 98336 | tf_op jit(solution)/shard_map/ppermute | solution.py:313
  68.1 28.5 %all-to-all-done.1.page_ref = bf16[64,24,512]{2,1,0:T(8,128)(2,1)S(1)} async-done(((bf16[64,24,512]{2,1,0:T(8,128)(2,1)}), bf16[64,24,512]{2,1,0:T(8,128)(2,1)S(1)}, u32[]{:S(2)}, u32[]{:S(2)}) %all-to-all-start.1) | async-done | bytes 1572896 | tf_op jit(solution)/shard_map/all_to_all | solution.py:25
  96.6 7.0 %forward_totals.1.refs_0_ = f32[24,1536]{1,0:T(8,128)S(1)} custom-call(bf16[1536,128]{1,0:T(8,128)(2,1)S(1)} %pad_maximum_fusion.2.q_ref, bf16[64,24,512]{2,1,0:T(8,128)(2,1)S(1)} %all-to-all-done.1.page_ref), custom_call_target="tpu_custom_call" | custom-call | flops 2415919104 | bytes 3145728 | tf_op jit(solution)/shard_map/forward_totals/pallas_call | solution.py:262
  103.6 2.8 %collective-permute-start.3 = (f32[24,1536]{1,0:T(8,128)S(1)}, f32[24,1536]{1,0:T(8,128)S(1)}, u32[]{:S(2)}, u32[]{:S(2)}) collective-permute-start(f32[24,1536]{1,0:T(8,128)S(1)} %forward_totals.1.refs_0_), channel_id=1, source_target_pairs={{1,0},{2,1},{3,2},{0,3},{5,4},{6,5},{7,6},{4,7},{9,8},{10,9},{11,1... | collective-permute-start | bytes 442376 | tf_op jit(solution)/shard_map/ppermute | solution.py:313
  106.8 0.7 collective-permute-start.5
  107.5 5.1 %collective-permute-done.3.refs_1_ = f32[24,1536]{1,0:T(8,128)S(1)} collective-permute-done((f32[24,1536]{1,0:T(8,128)S(1)}, f32[24,1536]{1,0:T(8,128)S(1)}, u32[]{:S(2)}, u32[]{:S(2)}) %collective-permute-start.3) | collective-permute-done | bytes 147488 | tf_op jit(solution)/shard_map/ppermute | solution.py:313
  113.0 3.8 %collective-permute-done.5.refs_3_ = f32[24,1536]{1,0:T(8,128)S(1)} collective-permute-done((f32[24,1536]{1,0:T(8,128)S(1)}, f32[24,1536]{1,0:T(8,128)S(1)}, u32[]{:S(2)}, u32[]{:S(2)}) %collective-permute-start.5) | collective-permute-done | bytes 147488 | tf_op jit(solution)/shard_map/ppermute | solution.py:313
  117.4 5.2 %page_side.3 = bf16[64,8,512]{2,1,0:T(8,128)(2,1)} custom-call(bf16[1536,128]{1,0:T(8,128)(2,1)S(1)} %pad_maximum_fusion.2.q_ref, bf16[64,24,512]{2,1,0:T(8,128)(2,1)S(1)} %all-to-all-done.1.page_ref, f32[24,1536]{1,0:T(8,128)S(1)} %get-tuple-element.11.weight_ref), custom_call_target="tpu_custom_call" | custom-call | flops 1610612736 | bytes 1048576 | tf_op jit(solution)/shard_map/page_side/pallas_call | solution.py:262
  122.6 6.1 %all-to-all-start.3 = ((bf16[64,8,512]{2,1,0:T(8,128)(2,1)}), bf16[64,8,512]{2,1,0:T(8,128)(2,1)S(1)}, u32[]{:S(2)}, u32[]{:S(2)}) async-start(bf16[64,8,512]{2,1,0:T(8,128)(2,1)} %page_side.3), calls=%async_computation.3 | async-start | bytes 1048576 | tf_op jit(solution)/shard_map/all_to_all | solution.py:25
  128.8 9.7 %page_side.2 = bf16[64,16,512]{2,1,0:T(8,128)(2,1)} custom-call(bf16[1536,128]{1,0:T(8,128)(2,1)S(1)} %pad_maximum_fusion.2.q_ref, bf16[64,24,512]{2,1,0:T(8,128)(2,1)S(1)} %all-to-all-done.1.page_ref, f32[24,1536]{1,0:T(8,128)S(1)} %get-tuple-element.11.weight_ref), custom_call_target="tpu_custom_call" | custom-call | flops 3221225472 | bytes 2097152 | tf_op jit(solution)/shard_map/page_side/pallas_call | solution.py:262
  138.4 7.6 %all-to-all-done.3 = bf16[64,8,512]{2,1,0:T(8,128)(2,1)S(1)} async-done(((bf16[64,8,512]{2,1,0:T(8,128)(2,1)}), bf16[64,8,512]{2,1,0:T(8,128)(2,1)S(1)}, u32[]{:S(2)}, u32[]{:S(2)}) %all-to-all-start.3) | async-done | bytes 524320 | tf_op jit(solution)/shard_map/all_to_all | solution.py:25
  146.0 0.8 copy-done.1
  146.9 6.5 %all-to-all-start.2 = ((bf16[64,16,512]{2,1,0:T(8,128)(2,1)}), bf16[64,16,512]{2,1,0:T(8,128)(2,1)}, u32[]{:S(2)}, u32[]{:S(2)}) async-start(bf16[64,16,512]{2,1,0:T(8,128)(2,1)} %page_side.2), calls=%async_computation.2 | async-start | bytes 2097152 | tf_op jit(solution)/shard_map/all_to_all | solution.py:25
  153.3 11.6 %query_side.1 = f32[1536,128]{1,0:T(8,128)S(1)} custom-call(bf16[1536,128]{1,0:T(8,128)(2,1)S(1)} %pad_maximum_fusion.2.q_ref, bf16[64,24,512]{2,1,0:T(8,128)(2,1)S(1)} %all-to-all-done.1.page_ref, f32[24,1536]{1,0:T(8,128)S(1)} %get-tuple-element.11.weight_ref), custom_call_target="tpu_custom_call" | custom-call | flops 4831838208 | bytes 3145728 | tf_op jit(solution)/shard_map/query_side/pallas_call | solution.py:262
  165.1 1.5 collective-permute-start.7
  166.6 1.2 collective-permute-start.8
  168.0 8.5 %collective-permute-done.6 = f32[384,128]{1,0:T(8,128)S(1)} collective-permute-done((f32[384,128]{1,0:T(8,128)S(1)}, f32[384,128]{1,0:T(8,128)S(1)}, u32[]{:S(2)}, u32[]{:S(2)}) %collective-permute-start.6) | collective-permute-done | bytes 196640 | tf_op jit(solution)/shard_map/ppermute | solution.py:313
  177.2 0.9 fusion.13
  178.1 3.7 %all-to-all-done.2 = bf16[64,16,512]{2,1,0:T(8,128)(2,1)} async-done(((bf16[64,16,512]{2,1,0:T(8,128)(2,1)}), bf16[64,16,512]{2,1,0:T(8,128)(2,1)}, u32[]{:S(2)}, u32[]{:S(2)}) %all-to-all-start.2) | async-done | bytes 1048608 | tf_op jit(solution)/shard_map/all_to_all | solution.py:25
  181.8 2.5 %fusion.1 = f32[1024,512]{1,0:T(8,128)S(1)} fusion(bf16[1024,512]{1,0:T(8,128)(2,1)} %bitcast.12, s32[1024]{0:T(1024)S(1)} %eq.54), kind=kOutput, calls=%fused_computation.3 | convolution fusion | flops 1074790400 | bytes 3149824 | tf_op jit(solution)/shard_map/dot_general | solution.py:375
  184.3 1.7 add_convert_fusion
  186.0 7.8 %all-to-all-start.4 = ((bf16[64,16,512]{2,1,0:T(8,128)(2,1)}), bf16[64,16,512]{2,1,0:T(8,128)(2,1)S(1)}, u32[]{:S(2)}, u32[]{:S(2)}) async-start(bf16[64,16,512]{2,1,0:T(8,128)(2,1)} %bitcast.13), calls=%async_computation.4 | async-start | bytes 2097152 | tf_op jit(solution)/shard_map/all_to_all | solution.py:25
  193.9 0.6 copy.11
  194.5 27.8 %all-to-all-done.4.page_ref = bf16[64,16,512]{2,1,0:T(8,128)(2,1)S(1)} async-done(((bf16[64,16,512]{2,1,0:T(8,128)(2,1)}), bf16[64,16,512]{2,1,0:T(8,128)(2,1)S(1)}, u32[]{:S(2)}, u32[]{:S(2)}) %all-to-all-start.4) | async-done | bytes 1048608 | tf_op jit(solution)/shard_map/all_to_all | solution.py:25
  222.3 1.7 page_order.1
  (40 shorter events, 4.5 us)
Async XLA Ops:
  0.6 1.9 copy-start.3
  0.6 2.0 copy-start.4
  50.5 6.3 %copy-start = (bf16[1,12,32,128]{3,2,1,0:T(8,128)(2,1)S(1)}, bf16[1,12,32,128]{3,2,1,0:T(8,128)(2,1)}, u32[]{:S(2)}) copy-start(bf16[1,12,32,128]{3,2,1,0:T(8,128)(2,1)} %param.4) | copy-start | bytes 294916
  50.5 46.1 %all-to-all-start.1 = ((bf16[64,24,512]{2,1,0:T(8,128)(2,1)}), bf16[64,24,512]{2,1,0:T(8,128)(2,1)S(1)}, u32[]{:S(2)}, u32[]{:S(2)}) async-start(bf16[64,24,512]{2,1,0:T(8,128)(2,1)} %bitcast.7), calls=%async_computation.1 | async-start | bytes 3145728 | tf_op jit(solution)/shard_map/all_to_all | solution.py:25
  57.1 4.4 %collective-permute-start = (bf16[384,128]{1,0:T(8,128)(2,1)S(1)}, bf16[384,128]{1,0:T(8,128)(2,1)S(1)}, u32[]{:S(2)}, u32[]{:S(2)}) collective-permute-start(bf16[384,128]{1,0:T(8,128)(2,1)S(1)} %fusion.14), channel_id=1, source_target_pairs={{1,0},{2,1},{3,2},{0,3},{5,4},{6,5},{7,6},{4,7},{9,8},{10,9},{11,1... | collective-permute-start | bytes 294920 | tf_op jit(solution)/shard_map/ppermute | solution.py:313
  59.9 5.3 %collective-permute-start.1 = (bf16[384,128]{1,0:T(8,128)(2,1)S(1)}, bf16[384,128]{1,0:T(8,128)(2,1)S(1)}, u32[]{:S(2)}, u32[]{:S(2)}) collective-permute-start(bf16[384,128]{1,0:T(8,128)(2,1)S(1)} %fusion.14), channel_id=1, source_target_pairs={{2,0},{3,1},{0,2},{1,3},{6,4},{7,5},{4,6},{5,7},{10,8},{11,9},{8,1... | collective-permute-start | bytes 294920 | tf_op jit(solution)/shard_map/ppermute | solution.py:313
  60.3 7.8 %collective-permute-start.2 = (bf16[384,128]{1,0:T(8,128)(2,1)S(1)}, bf16[384,128]{1,0:T(8,128)(2,1)S(1)}, u32[]{:S(2)}, u32[]{:S(2)}) collective-permute-start(bf16[384,128]{1,0:T(8,128)(2,1)S(1)} %fusion.14), channel_id=1, source_target_pairs={{3,0},{0,1},{1,2},{2,3},{7,4},{4,5},{5,6},{6,7},{11,8},{8,9},{9,10... | collective-permute-start | bytes 294920 | tf_op jit(solution)/shard_map/ppermute | solution.py:313
  103.6 9.0 %collective-permute-start.3 = (f32[24,1536]{1,0:T(8,128)S(1)}, f32[24,1536]{1,0:T(8,128)S(1)}, u32[]{:S(2)}, u32[]{:S(2)}) collective-permute-start(f32[24,1536]{1,0:T(8,128)S(1)} %forward_totals.1.refs_0_), channel_id=1, source_target_pairs={{1,0},{2,1},{3,2},{0,3},{5,4},{6,5},{7,6},{4,7},{9,8},{10,9},{11,1... | collective-permute-start | bytes 442376 | tf_op jit(solution)/shard_map/ppermute | solution.py:313
  106.4 6.6 %collective-permute-start.4 = (f32[24,1536]{1,0:T(8,128)S(1)}, f32[24,1536]{1,0:T(8,128)S(1)}, u32[]{:S(2)}, u32[]{:S(2)}) collective-permute-start(f32[24,1536]{1,0:T(8,128)S(1)} %forward_totals.1.refs_0_), channel_id=1, source_target_pairs={{2,0},{3,1},{0,2},{1,3},{6,4},{7,5},{4,6},{5,7},{10,8},{11,9},{8,1... | collective-permute-start | bytes 442376 | tf_op jit(solution)/shard_map/ppermute | solution.py:313
  106.8 10.1 %collective-permute-start.5 = (f32[24,1536]{1,0:T(8,128)S(1)}, f32[24,1536]{1,0:T(8,128)S(1)}, u32[]{:S(2)}, u32[]{:S(2)}) collective-permute-start(f32[24,1536]{1,0:T(8,128)S(1)} %forward_totals.1.refs_0_), channel_id=1, source_target_pairs={{3,0},{0,1},{1,2},{2,3},{7,4},{4,5},{5,6},{6,7},{11,8},{8,9},{9,10... | collective-permute-start | bytes 442376 | tf_op jit(solution)/shard_map/ppermute | solution.py:313
  122.6 23.4 %all-to-all-start.3 = ((bf16[64,8,512]{2,1,0:T(8,128)(2,1)}), bf16[64,8,512]{2,1,0:T(8,128)(2,1)S(1)}, u32[]{:S(2)}, u32[]{:S(2)}) async-start(bf16[64,8,512]{2,1,0:T(8,128)(2,1)} %page_side.3), calls=%async_computation.3 | async-start | bytes 1048576 | tf_op jit(solution)/shard_map/all_to_all | solution.py:25
  146.0 0.8 copy-start.1
  146.9 34.9 %all-to-all-start.2 = ((bf16[64,16,512]{2,1,0:T(8,128)(2,1)}), bf16[64,16,512]{2,1,0:T(8,128)(2,1)}, u32[]{:S(2)}, u32[]{:S(2)}) async-start(bf16[64,16,512]{2,1,0:T(8,128)(2,1)} %page_side.2), calls=%async_computation.2 | async-start | bytes 2097152 | tf_op jit(solution)/shard_map/all_to_all | solution.py:25
  165.0 11.5 %collective-permute-start.6 = (f32[384,128]{1,0:T(8,128)S(1)}, f32[384,128]{1,0:T(8,128)S(1)}, u32[]{:S(2)}, u32[]{:S(2)}) collective-permute-start(f32[384,128]{1,0:T(8,128)S(1)} %get-tuple-element.21), channel_id=1, source_target_pairs={{3,0},{0,1},{1,2},{2,3},{7,4},{4,5},{5,6},{6,7},{11,8},{8,9},{9,10... | collective-permute-start | bytes 589832 | tf_op jit(solution)/shard_map/ppermute | solution.py:313
  165.1 11.5 %collective-permute-start.7 = (f32[384,128]{1,0:T(8,128)S(1)}, f32[384,128]{1,0:T(8,128)S(1)}, u32[]{:S(2)}, u32[]{:S(2)}) collective-permute-start(f32[384,128]{1,0:T(8,128)S(1)} %get-tuple-element.23), channel_id=1, source_target_pairs={{2,0},{3,1},{0,2},{1,3},{6,4},{7,5},{4,6},{5,7},{10,8},{11,9},{8,1... | collective-permute-start | bytes 589832 | tf_op jit(solution)/shard_map/ppermute | solution.py:313
  166.6 10.3 %collective-permute-start.8 = (f32[384,128]{1,0:T(8,128)S(1)}, f32[384,128]{1,0:T(8,128)S(1)}, u32[]{:S(2)}, u32[]{:S(2)}) collective-permute-start(f32[384,128]{1,0:T(8,128)S(1)} %get-tuple-element.22), channel_id=1, source_target_pairs={{1,0},{2,1},{3,2},{0,3},{5,4},{6,5},{7,6},{4,7},{9,8},{10,9},{11,1... | collective-permute-start | bytes 589832 | tf_op jit(solution)/shard_map/ppermute | solution.py:313
  181.8 2.5 %copy-start.2 = (bf16[64,8,512]{2,1,0:T(8,128)(2,1)S(1)}, bf16[64,8,512]{2,1,0:T(8,128)(2,1)}, u32[]{:S(2)}) copy-start(bf16[64,8,512]{2,1,0:T(8,128)(2,1)} %copy-done.1) | copy-start | bytes 1572868
  186.0 36.3 %all-to-all-start.4 = ((bf16[64,16,512]{2,1,0:T(8,128)(2,1)}), bf16[64,16,512]{2,1,0:T(8,128)(2,1)S(1)}, u32[]{:S(2)}, u32[]{:S(2)}) async-start(bf16[64,16,512]{2,1,0:T(8,128)(2,1)} %bitcast.13), calls=%async_computation.4 | async-start | bytes 2097152 | tf_op jit(solution)/shard_map/all_to_all | solution.py:25

commit v5 on v4

--- a/solution.py
+++ b/solution.py
@@ -15,7 +15,6 @@
 EXP2_SCALE = SHARPNESS * math.log2(math.e)
 PER_STEP = 8
 PER_LOOP = 4
-FIRST_CHUNK = 8
 PARAMS = pltpu.CompilerParams(vmem_limit_bytes=24 << 20)
 GRAD_TYPE = jnp.bfloat16
 OWN_TYPE = jnp.bfloat16
@@ -160,12 +159,12 @@
         fill(q_ref, raw_ref, unit_ref, turn, per_step, use)
 
 
-def page_side_kernel(offset, q_ref, page_ref, weight_ref, grad_ref, raw_ref, unit_ref, share_ref):
+def page_side_kernel(q_ref, page_ref, weight_ref, grad_ref, raw_ref, unit_ref, share_ref):
     per_step = page_ref.shape[1]
     pieces = page_ref.shape[0]
     depth, _, width = raw_ref.shape
     load_pages(page_ref, raw_ref)
-    step_first = offset + pl.program_id(0) * per_step
+    step_first = pl.program_id(0) * per_step
 
     @pl.loop(0, per_step // math.gcd(per_step, PER_LOOP))
     def _(turn):
@@ -240,15 +239,11 @@
 
 
 def over_candidates(
-    kernel, name, products, query_rows, fetched, weights, out_spec, out_shape, back, window=None
+    kernel, name, products, query_rows, fetched, weights, out_spec, out_shape, back
 ):
     rows, width = query_rows.shape
     pieces, candidates, wide = fetched.shape
     per_step = math.gcd(candidates, PER_STEP)
-    first_step = 0
-    if window:
-        per_step = math.gcd(*window, per_step)
-        first_step, candidates = window[0] // per_step, window[1]
     together = math.gcd(per_step, PER_LOOP)
     patches = pieces * wide // width
     scratch = [
@@ -264,7 +259,7 @@
         grid=(candidates // per_step,),
         in_specs=[
             pl.BlockSpec((rows, width), lambda i: (0, 0)),
-            pl.BlockSpec((pieces, per_step, wide), lambda i: (0, i + first_step, 0)),
+            pl.BlockSpec((pieces, per_step, wide), lambda i: (0, i, 0)),
         ]
         + [pl.BlockSpec(table.shape, lambda i: (0, 0)) for table in weights],
         out_specs=out_spec,
@@ -288,14 +283,13 @@
     )
 
 
-def page_side(query_rows, fetched, weights, window):
+def page_side(query_rows, fetched, weights):
     pieces, candidates, wide = fetched.shape
-    per_step = math.gcd(*window, candidates, PER_STEP)
+    per_step = math.gcd(candidates, PER_STEP)
     spec = pl.BlockSpec((pieces, per_step, wide), lambda i: (0, i, 0))
-    shape = jax.ShapeDtypeStruct((pieces, window[1], wide), GRAD_TYPE)
-    kernel = functools.partial(page_side_kernel, window[0])
+    shape = jax.ShapeDtypeStruct(fetched.shape, GRAD_TYPE)
     return over_candidates(
-        kernel, "page_side", 2, query_rows, fetched, [weights], spec, shape, False, window
+        page_side_kernel, "page_side", 2, query_rows, fetched, [weights], spec, shape, False
     )
 
 
@@ -352,12 +346,7 @@
     weights, row_losses = weights_of([totals], [k * rows_local for k in range(group)], tokens)
     losses = row_losses[0, :rows_local].reshape(queries_local, tokens)[:, 0]
 
-    edge = FIRST_CHUNK if candidates > FIRST_CHUNK else candidates // 2
-    windows = ((0, edge), (edge, candidates - edge))
-    terms = [page_side(query_rows, fetched, weights, windows[0])]
-    terms.append(page_side(query_rows, fetched, weights, windows[1]))
-    returned = [exchange(part, "pages") for part in terms]
-    returned[0], weights = lax.optimization_barrier((returned[0], weights))
+    returned = exchange(page_side(query_rows, fetched, weights), "pages")
 
     grad_rows = query_side(query_rows, fetched, weights).reshape(group, rows_local, width)
     own_grads = grad_rows[0]
@@ -366,15 +355,10 @@
     query_grad = unnormalize_grad(
         q_unit, q_inv, own_grads.reshape(queries_local, tokens, width)
     )
-    returned[1], query_grad = lax.optimization_barrier((returned[1], query_grad))
-
-    summed = 0.0
-    for part, (low, count) in zip(returned, windows):
-        rows = asked[:, low : low + count].reshape(-1)
-        collector = (page_range[:, None] == rows[None, :]).astype(GRAD_TYPE)
-        summed = summed + jnp.dot(
-            collector, part.reshape(-1, wide), preferred_element_type=jnp.float32
-        )
+    returned, query_grad = lax.optimization_barrier((returned, query_grad))
+
+    collector = (page_range[:, None] == asked.reshape(-1)[None, :]).astype(GRAD_TYPE)
+    summed = jnp.dot(collector, returned.reshape(-1, wide), preferred_element_type=jnp.float32)
     own = exchange(summed.astype(OWN_TYPE).reshape(owners_count, local_pages, wide), "pages")
     page_grad = in_page_order(own, width)
     return (losses[None, :], query_grad[None], page_grad)

time: 225 us -> 218 us (0.969)
  starting transfers between devices: 37.1 us -> 29.1 us
  waiting for transfers between devices: 93 us -> 96.8 us
    all_to_all x4 -> x3, starting transfers between devices: 26.7 us -> 18.7 us  [exchange(): return lax.all_to_all(value, axis, split_axis=0, concat_axis=0, tiled=True)]
    all_to_all x4 -> x3, waiting for transfers between devices: 67.6 us -> 71.2 us  [exchange(): return lax.all_to_all(value, axis, split_axis=0, concat_axis=0, tiled=True)]
    pallas_call x4 -> x3, Pallas kernels: 33.5 us -> 32.8 us  [over_candidates(): pl.pallas_call(kernel, grid=(candidates // per_step,), in_specs=[pl.Block...]
  transfers between devices with their start and end apart: 13 -> 12, of which waited for: 12 -> 11; matrix products, arithmetic and copies ran while one was open for 1% -> 1% of each run, Pallas kernels for 10% -> 5%
where the time goes in v5:
time: 218 us
  waiting for transfers between devices  96.8 us (44%)
  blocking collectives  44.1 us (20%)
  Pallas kernels  35 us (16%)
  starting transfers between devices  29.1 us (13%)
  matrix products  7.19 us (3%)
  local copies, waits for them, and re-layouts  3.11 us (1%)
    all_to_all x3, waiting for transfers between devices, exchange(): return lax.all_to_all(value, axis, split_axis=0, concat_axis=0, tiled=True)  71.2 us
    all_to_all x1, blocking collectives, exchange(): return lax.all_to_all(value, axis, split_axis=0, concat_axis=0, tiled=True)  44.1 us
    pallas_call x3, Pallas kernels, over_candidates(): pl.pallas_call(kernel, grid=(candidates // per_step,), in_specs=[pl.Block...  32.8 us
    ppermute x9, waiting for transfers between devices, from_ahead(): return lax.ppermute(value, axis, pairs)  25.6 us
    all_to_all x3, starting transfers between devices, exchange(): return lax.all_to_all(value, axis, split_axis=0, concat_axis=0, tiled=True)  18.7 us
    ppermute x9, starting transfers between devices, from_ahead(): return lax.ppermute(value, axis, pairs)  10.5 us
  transfers between devices with their start and end apart: 12, of which 11 were waited for; matrix products, arithmetic and copies ran while one was open for 1% of the time, Pallas kernels for 5%

profile of v5, /device:TPU:1, one launch (start us, length us, event | category | flops | bytes accessed | tf_op | source)
XLA Modules:
  0.0 218.0 jit_solution(3183024509191711891)
XLA Ops:
  0.7 1.9 copy.9
  2.8 44.1 %all_to_all.20 = bf16[64,72,128]{2,1,0:T(8,128)(2,1)S(1)} all-to-all(bf16[64,72,128]{2,1,0:T(8,128)(2,1)S(1)} %pad_maximum_fusion), channel_id=1, replica_groups=mesh['pages'=64,'query'=4] {'pages'}, dimensions={0} | all-to-all | bytes 2359296 | tf_op jit(solution)/shard_map/all_to_all | solution.py:24
  47.5 3.0 %fusion.4 = bf16[1536,512]{1,0:T(8,128)(2,1)} fusion(bf16[1024,512]{1,0:T(8,128)(2,1)S(1)} %bitcast.34, s32[1536]{0:T(1024)S(1)} %eq.28), kind=kOutput, calls=%fused_computation.6 | convolution fusion | flops 1612972032 | bytes 2627584 | tf_op jit(solution)/shard_map/dot_general | solution.py:341
  50.5 6.3 %all-to-all-start.1 = ((bf16[64,24,512]{2,1,0:T(8,128)(2,1)}), bf16[64,24,512]{2,1,0:T(8,128)(2,1)S(1)}, u32[]{:S(2)}, u32[]{:S(2)}) async-start(bf16[64,24,512]{2,1,0:T(8,128)(2,1)} %bitcast.7), calls=%async_computation.1 | async-start | bytes 3145728 | tf_op jit(solution)/shard_map/all_to_all | solution.py:24
  57.1 2.8 %collective-permute-start = (bf16[384,128]{1,0:T(8,128)(2,1)S(1)}, bf16[384,128]{1,0:T(8,128)(2,1)S(1)}, u32[]{:S(2)}, u32[]{:S(2)}) collective-permute-start(bf16[384,128]{1,0:T(8,128)(2,1)S(1)} %fusion.12), channel_id=1, source_target_pairs={{1,0},{2,1},{3,2},{0,3},{5,4},{6,5},{7,6},{4,7},{9,8},{10,9},{11,1... | collective-permute-start | bytes 294920 | tf_op jit(solution)/shard_map/ppermute | solution.py:307
  60.0 0.3 collective-permute-start.1
  60.3 0.7 collective-permute-start.2
  61.0 0.6 collective-permute-done
  61.6 3.6 %collective-permute-done.1 = bf16[384,128]{1,0:T(8,128)(2,1)S(1)} collective-permute-done((bf16[384,128]{1,0:T(8,128)(2,1)S(1)}, bf16[384,128]{1,0:T(8,128)(2,1)S(1)}, u32[]{:S(2)}, u32[]{:S(2)}) %collective-permute-start.1) | collective-permute-done | bytes 98336 | tf_op jit(solution)/shard_map/ppermute | solution.py:307
  65.2 2.9 %collective-permute-done.2 = bf16[384,128]{1,0:T(8,128)(2,1)S(1)} collective-permute-done((bf16[384,128]{1,0:T(8,128)(2,1)S(1)}, bf16[384,128]{1,0:T(8,128)(2,1)S(1)}, u32[]{:S(2)}, u32[]{:S(2)}) %collective-permute-start.2) | collective-permute-done | bytes 98336 | tf_op jit(solution)/shard_map/ppermute | solution.py:307
  68.1 28.4 %all-to-all-done.1.page_ref = bf16[64,24,512]{2,1,0:T(8,128)(2,1)S(1)} async-done(((bf16[64,24,512]{2,1,0:T(8,128)(2,1)}), bf16[64,24,512]{2,1,0:T(8,128)(2,1)S(1)}, u32[]{:S(2)}, u32[]{:S(2)}) %all-to-all-start.1) | async-done | bytes 1572896 | tf_op jit(solution)/shard_map/all_to_all | solution.py:24
  96.5 7.1 %forward_totals.1.refs_0_ = f32[24,1536]{1,0:T(8,128)S(1)} custom-call(bf16[1536,128]{1,0:T(8,128)(2,1)S(1)} %pad_maximum_fusion.2.q_ref, bf16[64,24,512]{2,1,0:T(8,128)(2,1)S(1)} %all-to-all-done.1.page_ref), custom_call_target="tpu_custom_call" | custom-call | flops 2415919104 | bytes 3145728 | tf_op jit(solution)/shard_map/forward_totals/pallas_call | solution.py:257
  103.6 2.8 %collective-permute-start.3 = (f32[24,1536]{1,0:T(8,128)S(1)}, f32[24,1536]{1,0:T(8,128)S(1)}, u32[]{:S(2)}, u32[]{:S(2)}) collective-permute-start(f32[24,1536]{1,0:T(8,128)S(1)} %forward_totals.1.refs_0_), channel_id=1, source_target_pairs={{1,0},{2,1},{3,2},{0,3},{5,4},{6,5},{7,6},{4,7},{9,8},{10,9},{11,1... | collective-permute-start | bytes 442376 | tf_op jit(solution)/shard_map/ppermute | solution.py:307
  106.8 0.7 collective-permute-start.5
  107.5 5.1 %collective-permute-done.3.refs_1_ = f32[24,1536]{1,0:T(8,128)S(1)} collective-permute-done((f32[24,1536]{1,0:T(8,128)S(1)}, f32[24,1536]{1,0:T(8,128)S(1)}, u32[]{:S(2)}, u32[]{:S(2)}) %collective-permute-start.3) | collective-permute-done | bytes 147488 | tf_op jit(solution)/shard_map/ppermute | solution.py:307
  112.6 0.5 collective-permute-done.4.refs_2_
  113.0 3.8 %collective-permute-done.5.refs_3_ = f32[24,1536]{1,0:T(8,128)S(1)} collective-permute-done((f32[24,1536]{1,0:T(8,128)S(1)}, f32[24,1536]{1,0:T(8,128)S(1)}, u32[]{:S(2)}, u32[]{:S(2)}) %collective-permute-start.5) | collective-permute-done | bytes 147488 | tf_op jit(solution)/shard_map/ppermute | solution.py:307
  116.9 0.6 weights.1
  117.4 14.1 %page_side.1 = bf16[64,24,512]{2,1,0:T(8,128)(2,1)} custom-call(bf16[1536,128]{1,0:T(8,128)(2,1)S(1)} %pad_maximum_fusion.2.q_ref, bf16[64,24,512]{2,1,0:T(8,128)(2,1)S(1)} %all-to-all-done.1.page_ref, f32[24,1536]{1,0:T(8,128)S(1)} %get-tuple-element.8.weight_ref), custom_call_target="tpu_custom_call" | custom-call | flops 4831838208 | bytes 3145728 | tf_op jit(solution)/shard_map/page_side/pallas_call | solution.py:257
  131.6 6.3 %all-to-all-start.2 = ((bf16[64,24,512]{2,1,0:T(8,128)(2,1)}), bf16[64,24,512]{2,1,0:T(8,128)(2,1)}, u32[]{:S(2)}, u32[]{:S(2)}) async-start(bf16[64,24,512]{2,1,0:T(8,128)(2,1)} %page_side.1), calls=%async_computation.2 | async-start | bytes 3145728 | tf_op jit(solution)/shard_map/all_to_all | solution.py:24
  137.9 11.6 %query_side.1 = f32[1536,128]{1,0:T(8,128)S(1)} custom-call(bf16[1536,128]{1,0:T(8,128)(2,1)S(1)} %pad_maximum_fusion.2.q_ref, bf16[64,24,512]{2,1,0:T(8,128)(2,1)S(1)} %all-to-all-done.1.page_ref, f32[24,1536]{1,0:T(8,128)S(1)} %get-tuple-element.8.weight_ref), custom_call_target="tpu_custom_call" | custom-call | flops 4831838208 | bytes 3145728 | tf_op jit(solution)/shard_map/query_side/pallas_call | solution.py:257
  149.6 1.5 collective-permute-start.7
  151.1 1.2 collective-permute-start.8
  152.3 8.8 %collective-permute-done.6 = f32[384,128]{1,0:T(8,128)S(1)} collective-permute-done((f32[384,128]{1,0:T(8,128)S(1)}, f32[384,128]{1,0:T(8,128)S(1)}, u32[]{:S(2)}, u32[]{:S(2)}) %collective-permute-start.6) | collective-permute-done | bytes 196640 | tf_op jit(solution)/shard_map/ppermute | solution.py:307
  161.1 0.4 collective-permute-done.8
  161.7 0.9 fusion.11
  162.6 15.0 %all-to-all-done.2 = bf16[64,24,512]{2,1,0:T(8,128)(2,1)} async-done(((bf16[64,24,512]{2,1,0:T(8,128)(2,1)}), bf16[64,24,512]{2,1,0:T(8,128)(2,1)}, u32[]{:S(2)}, u32[]{:S(2)}) %all-to-all-start.2) | async-done | bytes 1572896 | tf_op jit(solution)/shard_map/all_to_all | solution.py:24
  177.6 4.2 %fusion.5 = bf16[1024,512]{1,0:T(8,128)(2,1)} fusion(bf16[1536,512]{1,0:T(8,128)(2,1)} %bitcast.11, s32[1536]{0:T(1024)S(1)} %eq.28), kind=kOutput, calls=%fused_computation.7 | convolution fusion | flops 1612709888 | bytes 2627584 | tf_op jit(solution)/shard_map/dot_general | solution.py:361
  181.7 6.1 %all-to-all-start.3 = ((bf16[64,16,512]{2,1,0:T(8,128)(2,1)}), bf16[64,16,512]{2,1,0:T(8,128)(2,1)S(1)}, u32[]{:S(2)}, u32[]{:S(2)}) async-start(bf16[64,16,512]{2,1,0:T(8,128)(2,1)} %bitcast.12), calls=%async_computation.3 | async-start | bytes 2097152 | tf_op jit(solution)/shard_map/all_to_all | solution.py:24
  187.9 0.6 copy.11
  188.5 27.8 %all-to-all-done.3.page_ref = bf16[64,16,512]{2,1,0:T(8,128)(2,1)S(1)} async-done(((bf16[64,16,512]{2,1,0:T(8,128)(2,1)}), bf16[64,16,512]{2,1,0:T(8,128)(2,1)S(1)}, u32[]{:S(2)}, u32[]{:S(2)}) %all-to-all-start.3) | async-done | bytes 1048608 | tf_op jit(solution)/shard_map/all_to_all | solution.py:24
  216.4 1.7 page_order.1
  (29 shorter events, 2.0 us)
Async XLA Ops:
  0.6 1.9 copy-start.1
  0.6 2.0 copy-start.2
  50.5 6.3 %copy-start = (bf16[1,12,32,128]{3,2,1,0:T(8,128)(2,1)S(1)}, bf16[1,12,32,128]{3,2,1,0:T(8,128)(2,1)}, u32[]{:S(2)}) copy-start(bf16[1,12,32,128]{3,2,1,0:T(8,128)(2,1)} %param.4) | copy-start | bytes 294916
  50.5 46.1 %all-to-all-start.1 = ((bf16[64,24,512]{2,1,0:T(8,128)(2,1)}), bf16[64,24,512]{2,1,0:T(8,128)(2,1)S(1)}, u32[]{:S(2)}, u32[]{:S(2)}) async-start(bf16[64,24,512]{2,1,0:T(8,128)(2,1)} %bitcast.7), calls=%async_computation.1 | async-start | bytes 3145728 | tf_op jit(solution)/shard_map/all_to_all | solution.py:24
  57.1 4.5 %collective-permute-start = (bf16[384,128]{1,0:T(8,128)(2,1)S(1)}, bf16[384,128]{1,0:T(8,128)(2,1)S(1)}, u32[]{:S(2)}, u32[]{:S(2)}) collective-permute-start(bf16[384,128]{1,0:T(8,128)(2,1)S(1)} %fusion.12), channel_id=1, source_target_pairs={{1,0},{2,1},{3,2},{0,3},{5,4},{6,5},{7,6},{4,7},{9,8},{10,9},{11,1... | collective-permute-start | bytes 294920 | tf_op jit(solution)/shard_map/ppermute | solution.py:307
  60.0 5.3 %collective-permute-start.1 = (bf16[384,128]{1,0:T(8,128)(2,1)S(1)}, bf16[384,128]{1,0:T(8,128)(2,1)S(1)}, u32[]{:S(2)}, u32[]{:S(2)}) collective-permute-start(bf16[384,128]{1,0:T(8,128)(2,1)S(1)} %fusion.12), channel_id=1, source_target_pairs={{2,0},{3,1},{0,2},{1,3},{6,4},{7,5},{4,6},{5,7},{10,8},{11,9},{8,1... | collective-permute-start | bytes 294920 | tf_op jit(solution)/shard_map/ppermute | solution.py:307
  60.3 7.8 %collective-permute-start.2 = (bf16[384,128]{1,0:T(8,128)(2,1)S(1)}, bf16[384,128]{1,0:T(8,128)(2,1)S(1)}, u32[]{:S(2)}, u32[]{:S(2)}) collective-permute-start(bf16[384,128]{1,0:T(8,128)(2,1)S(1)} %fusion.12), channel_id=1, source_target_pairs={{3,0},{0,1},{1,2},{2,3},{7,4},{4,5},{5,6},{6,7},{11,8},{8,9},{9,10... | collective-permute-start | bytes 294920 | tf_op jit(solution)/shard_map/ppermute | solution.py:307
  103.6 9.0 %collective-permute-start.3 = (f32[24,1536]{1,0:T(8,128)S(1)}, f32[24,1536]{1,0:T(8,128)S(1)}, u32[]{:S(2)}, u32[]{:S(2)}) collective-permute-start(f32[24,1536]{1,0:T(8,128)S(1)} %forward_totals.1.refs_0_), channel_id=1, source_target_pairs={{1,0},{2,1},{3,2},{0,3},{5,4},{6,5},{7,6},{4,7},{9,8},{10,9},{11,1... | collective-permute-start | bytes 442376 | tf_op jit(solution)/shard_map/ppermute | solution.py:307
  106.4 6.6 %collective-permute-start.4 = (f32[24,1536]{1,0:T(8,128)S(1)}, f32[24,1536]{1,0:T(8,128)S(1)}, u32[]{:S(2)}, u32[]{:S(2)}) collective-permute-start(f32[24,1536]{1,0:T(8,128)S(1)} %forward_totals.1.refs_0_), channel_id=1, source_target_pairs={{2,0},{3,1},{0,2},{1,3},{6,4},{7,5},{4,6},{5,7},{10,8},{11,9},{8,1... | collective-permute-start | bytes 442376 | tf_op jit(solution)/shard_map/ppermute | solution.py:307
  106.8 10.1 %collective-permute-start.5 = (f32[24,1536]{1,0:T(8,128)S(1)}, f32[24,1536]{1,0:T(8,128)S(1)}, u32[]{:S(2)}, u32[]{:S(2)}) collective-permute-start(f32[24,1536]{1,0:T(8,128)S(1)} %forward_totals.1.refs_0_), channel_id=1, source_target_pairs={{3,0},{0,1},{1,2},{2,3},{7,4},{4,5},{5,6},{6,7},{11,8},{8,9},{9,10... | collective-permute-start | bytes 442376 | tf_op jit(solution)/shard_map/ppermute | solution.py:307
  131.6 46.0 %all-to-all-start.2 = ((bf16[64,24,512]{2,1,0:T(8,128)(2,1)}), bf16[64,24,512]{2,1,0:T(8,128)(2,1)}, u32[]{:S(2)}, u32[]{:S(2)}) async-start(bf16[64,24,512]{2,1,0:T(8,128)(2,1)} %page_side.1), calls=%async_computation.2 | async-start | bytes 3145728 | tf_op jit(solution)/shard_map/all_to_all | solution.py:24
  149.5 11.5 %collective-permute-start.6 = (f32[384,128]{1,0:T(8,128)S(1)}, f32[384,128]{1,0:T(8,128)S(1)}, u32[]{:S(2)}, u32[]{:S(2)}) collective-permute-start(f32[384,128]{1,0:T(8,128)S(1)} %get-tuple-element.17), channel_id=1, source_target_pairs={{3,0},{0,1},{1,2},{2,3},{7,4},{4,5},{5,6},{6,7},{11,8},{8,9},{9,10... | collective-permute-start | bytes 589832 | tf_op jit(solution)/shard_map/ppermute | solution.py:307
  149.6 11.5 %collective-permute-start.7 = (f32[384,128]{1,0:T(8,128)S(1)}, f32[384,128]{1,0:T(8,128)S(1)}, u32[]{:S(2)}, u32[]{:S(2)}) collective-permute-start(f32[384,128]{1,0:T(8,128)S(1)} %get-tuple-element.19), channel_id=1, source_target_pairs={{2,0},{3,1},{0,2},{1,3},{6,4},{7,5},{4,6},{5,7},{10,8},{11,9},{8,1... | collective-permute-start | bytes 589832 | tf_op jit(solution)/shard_map/ppermute | solution.py:307
  151.1 10.3 %collective-permute-start.8 = (f32[384,128]{1,0:T(8,128)S(1)}, f32[384,128]{1,0:T(8,128)S(1)}, u32[]{:S(2)}, u32[]{:S(2)}) collective-permute-start(f32[384,128]{1,0:T(8,128)S(1)} %get-tuple-element.18), channel_id=1, source_target_pairs={{1,0},{2,1},{3,2},{0,3},{5,4},{6,5},{7,6},{4,7},{9,8},{10,9},{11,1... | collective-permute-start | bytes 589832 | tf_op jit(solution)/shard_map/ppermute | solution.py:307
  181.7 34.6 %all-to-all-start.3 = ((bf16[64,16,512]{2,1,0:T(8,128)(2,1)}), bf16[64,16,512]{2,1,0:T(8,128)(2,1)S(1)}, u32[]{:S(2)}, u32[]{:S(2)}) async-start(bf16[64,16,512]{2,1,0:T(8,128)(2,1)} %bitcast.12), calls=%async_computation.3 | async-start | bytes 2097152 | tf_op jit(solution)/shard_map/all_to_all | solution.py:24
